TPU v7x, 128 devices: a whole 4x4x4 slice. The times are simulated.
128 devices in a mesh: lat: 8 (over y_hi, z), lon: 16 (over x, y_lo, core).
Axes of the slice: x: 4, y: 4 (y_hi: 2, y_lo: 2; y = y_hi * 2 + y_lo), z: 4, core: 2. Of those that a mesh axis runs over, the one named last changes fastest.
Arguments:
- fields: bfloat16 [2, 256, 768, 256], P(None, 'lat', 'lon'), may hold values from -6 to 6
- kernel: bfloat16 [9, 256, 256], replicated, may hold values from -0.125 to 0.125
- conv_bias: float32 [256], replicated, may hold values from -3 to 3
- cotangent: bfloat16 [2, 128, 384, 256], P(None, 'lat', 'lon'), may hold values from -6 to 6
Outputs:
- pooled: bfloat16 [2, 128, 384, 256], P(None, 'lat', 'lon')
- grad_input: bfloat16 [2, 256, 768, 256], P(None, 'lat', 'lon')
- grad_kernel: float32 [9, 256, 256], replicated
- grad_bias: float32 [256], replicated
All inputs are finite; a program needn't handle non-finite values.
Results may differ from a plain program's by a relative error of at most 0.013.
Values may be sent and summed in bfloat16 or wider, within the bound.
No kernel may reach another device: no remote copies, remote signals or barrier semaphores. Data moves between devices by JAX's collectives and lax.ppermute only.
A program may use at most 64 MiB of HBM per device.

v0:
```python
import math

import jax
import jax.numpy as jnp
from jax import lax
from jax.sharding import PartitionSpec as P


def shifted(shard, axis, by):
    size = lax.axis_size(axis)
    return lax.ppermute(shard, axis, [(i, (i + by) % size) for i in range(size)])


def with_halo(shard, sides, width, wrap):
    for axis, dim in sides:
        size, length = (lax.axis_size(axis), shard.shape[dim])
        up = [(i, (i + 1) % size) for i in range(size if wrap else size - 1)]
        down = [(j, i) for i, j in up]
        last = lax.slice_in_dim(shard, length - width, length, axis=dim)
        first = lax.slice_in_dim(shard, 0, width, axis=dim)
        before = lax.ppermute(last, axis, up)
        after = lax.ppermute(first, axis, down)
        shard = jnp.concatenate([before, shard, after], axis=dim)
    return shard


def lat_cosine(rows, first, total):
    index_rows = (first + jnp.arange(rows)).astype(jnp.float32)
    return jnp.cos((index_rows + 0.5) * (math.pi / total) - math.pi / 2)


def extend(field):
    lat_count = lax.axis_size("lat")
    lat_place = lax.axis_index("lat")
    lon_count = lax.axis_size("lon")
    north_row = field[:, :1]
    south_row = field[:, -1:]
    mirror_north, mirror_south = shifted((north_row, south_row), "lon", lon_count // 2)
    rim_rows = with_halo(field, (("lat", 1),), 1, False)
    upper_pad = jnp.where(lat_place == 0, mirror_north, rim_rows[:, :1])
    bottom = jnp.where(lat_place == lat_count - 1, mirror_south, rim_rows[:, -1:])
    tall = jnp.concatenate([upper_pad, field, bottom], axis=1)
    return with_halo(tall, (("lon", 2),), 1, True)


def forward_conv(padded, kernel, rows, cols):
    chans = padded.shape[-1]
    total = jnp.zeros((padded.shape[0] * rows * cols, kernel.shape[2]), jnp.float32)
    for row_off in range(3):
        for col_off in range(3):
            window = padded[:, row_off : row_off + rows, col_off : col_off + cols, :].reshape(
                -1, chans
            )
            total = total + jnp.dot(
                window, kernel[3 * row_off + col_off], preferred_element_type=jnp.float32
            )
    return total.reshape(padded.shape[0], rows, cols, kernel.shape[2])


def back_conv(padded, kernel, rows, cols):
    chans = padded.shape[-1]
    total = jnp.zeros((padded.shape[0] * rows * cols, kernel.shape[1]), jnp.float32)
    for row_off in range(3):
        for col_off in range(3):
            window = padded[
                :, 2 - row_off : 2 - row_off + rows, 2 - col_off : 2 - col_off + cols, :
            ].reshape(-1, chans)
            total = total + lax.dot_general(
                window,
                kernel[3 * row_off + col_off],
                (((1,), (1,)), ((), ())),
                preferred_element_type=jnp.float32,
            )
    return total.reshape(padded.shape[0], rows, cols, kernel.shape[1])


def pole_term(pad_row, kernel, row_off, cols):
    chans = pad_row.shape[-1]
    total = jnp.zeros((pad_row.shape[0] * cols, kernel.shape[1]), jnp.float32)
    for col_off in range(3):
        window = pad_row[:, :, 2 - col_off : 2 - col_off + cols, :].reshape(-1, chans)
        total = total + lax.dot_general(
            window,
            kernel[3 * row_off + col_off],
            (((1,), (1,)), ((), ())),
            preferred_element_type=jnp.float32,
        )
    return total.reshape(pad_row.shape[0], 1, cols, kernel.shape[1])


def kernel_grad(padded, grad_pre, rows, cols):
    chans = padded.shape[-1]
    flat_grad = grad_pre.reshape(-1, grad_pre.shape[-1])
    pieces = []
    for row_off in range(3):
        for col_off in range(3):
            window = padded[:, row_off : row_off + rows, col_off : col_off + cols, :].reshape(
                -1, chans
            )
            pieces.append(
                lax.dot_general(
                    window, flat_grad, (((0,), (0,)), ((), ())), preferred_element_type=jnp.float32
                )
            )
    return jnp.stack(pieces, axis=0)


def local(fields, kernel, conv_bias, cotangent):
    batches, rows, cols, chans = fields.shape
    lat_count = lax.axis_size("lat")
    lat_place = lax.axis_index("lat")
    padded = extend(fields)
    pre = forward_conv(padded, kernel, rows, cols) + conv_bias
    sigma = jax.nn.sigmoid(pre)
    active = (pre * sigma).astype(jnp.bfloat16)
    cosine = lat_cosine(rows, lat_place * rows, rows * lat_count)
    pair_sum = cosine[0::2] + cosine[1::2]
    weighted = active.astype(jnp.float32) * cosine[None, :, None, None]
    pooled = (
        weighted.reshape(batches, rows // 2, 2, cols // 2, 2, chans).sum(axis=(2, 4))
        / (2.0 * pair_sum)[None, :, None, None]
    )
    share = cosine / (2.0 * jnp.repeat(pair_sum, 2))
    spread = jnp.repeat(jnp.repeat(cotangent.astype(jnp.float32), 2, axis=1), 2, axis=2)
    grad_pre = (spread * share[None, :, None, None] * sigma * (1.0 + pre * (1.0 - sigma))).astype(
        jnp.bfloat16
    )
    kernel_part = kernel_grad(padded, grad_pre, rows, cols)
    bias_part = jnp.sum(grad_pre.astype(jnp.float32), axis=(0, 1, 2))
    grad_kernel, grad_bias = lax.psum((kernel_part, bias_part), ("lat", "lon"))
    grad_padded = extend(grad_pre)
    is_north = lat_place == 0
    is_south = lat_place == lat_count - 1
    blank = jnp.zeros_like(grad_padded[:, :1])
    upper_rows = jnp.where(is_north, blank, grad_padded[:, :1])
    lower_rows = jnp.where(is_south, blank, grad_padded[:, -1:])
    inner = jnp.concatenate([upper_rows, grad_padded[:, 1:-1], lower_rows], axis=1)
    back = back_conv(inner, kernel, rows, cols)
    north_add = jnp.where(is_north, pole_term(grad_padded[:, :1], kernel, 0, cols), 0.0)
    south_add = jnp.where(is_south, pole_term(grad_padded[:, -1:], kernel, 2, cols), 0.0)
    back = jnp.concatenate(
        [back[:, :1] + north_add, back[:, 1:-1], back[:, -1:] + south_add], axis=1
    )
    return (pooled.astype(jnp.bfloat16), back.astype(jnp.bfloat16), grad_kernel, grad_bias)


def solution(mesh):
    return jax.shard_map(
        local,
        mesh=mesh,
        in_specs=(P(None, "lat", "lon", None), P(), P(), P(None, "lat", "lon", None)),
        out_specs=(P(None, "lat", "lon", None), P(None, "lat", "lon", None), P(), P()),
        check_vma=False,
    )
```

profile of v0, /device:TPU:1, one launch (start us, length us, event | category | flops | bytes accessed | tf_op | source)
XLA Modules:
  0.0 244.1 jit_solution(9984950914171488139)
XLA Ops:
  8.0 3.6 %collective-permute-start.2 = (bf16[2,1,48,256]{3,2,1,0:T(8,128)(2,1)S(1)}, bf16[2,1,48,256]{3,2,1,0:T(8,128)(2,1)S(1)}, u32[]{:S(2)}, u32[]{:S(2)}) collective-permute-start(bf16[2,1,48,256]{3,2,1,0:T(8,128)(2,1)S(1)} %get-tuple-element.41), channel_id=1, source_target_pairs={{0,8},{1,9},{2,10},{3,11},{4,12},{5,13},{6,14},{7,15},{8,0},{9,1},... | collective-permute-start | bytes 147464 | tf_op jit(solution)/shard_map/ppermute | solution.py:11
  11.7 3.5 %collective-permute-start.1 = (bf16[2,1,48,256]{3,2,1,0:T(8,128)(2,1)S(1)}, bf16[2,1,48,256]{3,2,1,0:T(8,128)(2,1)S(1)}, u32[]{:S(2)}, u32[]{:S(2)}) collective-permute-start(bf16[2,1,48,256]{3,2,1,0:T(8,128)(2,1)S(1)} %get-tuple-element.41), channel_id=1, source_target_pairs={{0,16},{16,32},{32,48},{48,64},{64,80},{80,96},{96,112},{1,17},{17... | collective-permute-start | bytes 147464 | tf_op jit(solution)/shard_map/ppermute | solution.py:21
  18.5 1.7 broadcast_in_dim.22
  20.3 3.4 %reshape.184 = f32[3072,256]{1,0:T(8,128)} reshape(f32[2,32,24,2,256]{4,3,2,1,0:T(2,128)S(1)} %broadcast_in_dim.22) | data formatting | bytes 6291456 | tf_op jit(solution)/shard_map/reshape | solution.py:124
  23.7 3.4 %reshape.178 = f32[2,32,48,256]{3,2,1,0:T(8,128)} reshape(f32[2,32,24,2,256]{4,3,2,1,0:T(2,128)S(1)} %broadcast_in_dim.22) | data formatting | bytes 6291456 | tf_op jit(solution)/shard_map/reshape | solution.py:124
  28.8 1.6 collective-permute-start.5
  30.4 1.4 collective-permute-start.4
  34.9 3.1 %fusion.104 = (bf16[2,32,48,256]{3,2,1,0:T(8,128)(2,1)S(1)}, bf16[2,32,48,256]{3,2,1,0:T(8,128)(2,1)S(1)}, bf16[2,32,48,256]{3,2,1,0:T(8,128)(2,1)S(1)}, bf16[2,...) fusion(bf16[2,34,49,256]{3,2,1,0:T(8,128)(2,1)S(1)} %get-tuple-element., ...), kind=kLoop, calls=%fused_computation.171 | loop fusion | bytes 18874368 | tf_op jit(solution)/shard_map/slice | solution.py:51
  42.1 1.3 copy-done.10
  43.4 2.2 convert_reduce_fusion
  45.6 1.4 multiply_convert_fusion.2
  49.2 2.8 %collective-permute-start.6 = (bf16[2,1,48,256]{3,2,1,0:T(8,128)(2,1)}, bf16[2,1,48,256]{3,2,1,0:T(8,128)(2,1)}, u32[]{:S(2)}, u32[]{:S(2)}) collective-permute-start(bf16[2,1,48,256]{3,2,1,0:T(8,128)(2,1)} %get-tuple-element.37), channel_id=1, source_target_pairs={{0,8},{1,9},{2,10},{3,11},{4,12},{5,13},{6,14},{7,15},{8,0},{9,1},... | collective-permute-start | bytes 147464 | tf_op jit(solution)/shard_map/ppermute | solution.py:11
  52.3 5.4 %collective-permute-start.7 = (bf16[2,1,48,256]{3,2,1,0:T(8,128)(2,1)}, bf16[2,1,48,256]{3,2,1,0:T(8,128)(2,1)}, u32[]{:S(2)}, u32[]{:S(2)}) collective-permute-start(bf16[2,1,48,256]{3,2,1,0:T(8,128)(2,1)} %get-tuple-element.38), channel_id=1, source_target_pairs={{0,16},{16,32},{32,48},{48,64},{64,80},{80,96},{96,112},{1,17},{17... | collective-permute-start | bytes 147464 | tf_op jit(solution)/shard_map/ppermute | solution.py:21
  57.7 1.3 fusion.21
  59.0 5.2 %reshape.176 = f32[2,16,2,24,2,256]{5,4,3,2,1,0:T(2,128)} reshape(f32[3072,256]{1,0:T(8,128)} %copy-done.4) | data formatting | bytes 6291456 | tf_op jit(solution)/shard_map/reshape | solution.py:57
  64.2 2.8 %fusion.31 = f32[9,256,256]{2,1,0:T(8,128)} fusion(f32[9,256,256]{2,1,0:T(8,128)} %fusion.21, bf16[2,32,48,256]{3,2,1,0:T(8,128)(2,1)S(1)} %multiply_convert_fusion.2, bf16[2,32,48,256]{3,2,1,0:T(8,128)(2,1)} %param.4, bf16[2,1,48,256]{3,2,1,0:T(8,128)(2,1)} %copy-done.14), kind=kOutput, calls=%fused_computation.76 | convolution fusion | flops 405897216 | bytes 3457024 | tf_op jit(solution)/shard_map/dot_general | solution.py:101
  67.1 1.3 fusion.20
  68.4 1.3 fusion.19
  69.8 1.4 fusion.18
  71.3 1.3 fusion.17
  72.6 1.3 fusion.16
  73.9 1.3 fusion.25
  75.2 1.3 fusion.15
  77.3 3.2 %multiply_reduce_fusion = f32[2,16,24,256]{3,2,1,0:T(8,128)S(1)} fusion(f32[16,2]{1,0:T(8,128)S(1)} %add_cosine_fusion, f32[256]{0:T(256)S(1)} %copy-done.18, f32[2,16,2,24,2,256]{5,4,3,2,1,0:T(2,128)} %reshape.176), kind=kLoop, calls=%fused_computation.23 | loop fusion | flops 6881280 | bytes 3933312 | tf_op jit(solution)/shard_map/reduce_sum | solution.py:120
  81.4 72.1 %psum.15 = f32[256]{0:T(256)} all-reduce(f32[256]{0:T(256)S(1)} %copy-done.21), channel_id=1, replica_groups=mesh['lat'=8,'lon'=16] {'lat','lon'}, use_global_device_ids=true, to_apply=%region_3.4 | all-reduce | flops 256 | bytes 2048 | tf_op jit(solution)/shard_map/psum | solution.py:130
  156.3 1.6 collective-permute-start.10
  158.1 1.5 collective-permute-done.11
  163.7 2.1 pad_maximum_fusion.3
  170.5 1.5 convolution_add_fusion.4
  175.5 1.3 pad_maximum_fusion.7
  176.8 57.3 %all-reduce.2.cloned.1.call-done = f32[9,256,256]{2,1,0:T(8,128)} async-done(((f32[9,256,256]{2,1,0:T(8,128)}), f32[9,256,256]{2,1,0:T(8,128)}) %all-reduce.2.cloned.1.call-update) | async-done | bytes 2359312 | tf_op jit(solution)/shard_map/psum | solution.py:130
  234.1 3.2 %copy.45 = f32[9,256,256]{2,1,0:T(8,128)} copy(f32[9,256,256]{2,1,0:T(8,128)} %all-reduce.2.cloned.1.call-done) | data formatting | bytes 4718592
  (117 shorter events, 32.1 us)
Async XLA Ops:
  7.2 226.9 %all-reduce.2.cloned.1.call-start = ((), (), s32[]{:S(2)}) async-start(), calls=%async_computation | async-start | bytes 4718592 | tf_op jit(solution)/shard_map/psum | solution.py:130
  8.0 19.7 %collective-permute-start.2 = (bf16[2,1,48,256]{3,2,1,0:T(8,128)(2,1)S(1)}, bf16[2,1,48,256]{3,2,1,0:T(8,128)(2,1)S(1)}, u32[]{:S(2)}, u32[]{:S(2)}) collective-permute-start(bf16[2,1,48,256]{3,2,1,0:T(8,128)(2,1)S(1)} %get-tuple-element.41), channel_id=1, source_target_pairs={{0,8},{1,9},{2,10},{3,11},{4,12},{5,13},{6,14},{7,15},{8,0},{9,1},... | collective-permute-start | bytes 147464 | tf_op jit(solution)/shard_map/ppermute | solution.py:11
  11.7 16.1 %collective-permute-start.1 = (bf16[2,1,48,256]{3,2,1,0:T(8,128)(2,1)S(1)}, bf16[2,1,48,256]{3,2,1,0:T(8,128)(2,1)S(1)}, u32[]{:S(2)}, u32[]{:S(2)}) collective-permute-start(bf16[2,1,48,256]{3,2,1,0:T(8,128)(2,1)S(1)} %get-tuple-element.41), channel_id=1, source_target_pairs={{0,16},{16,32},{32,48},{48,64},{64,80},{80,96},{96,112},{1,17},{17... | collective-permute-start | bytes 147464 | tf_op jit(solution)/shard_map/ppermute | solution.py:21
  15.2 12.5 %collective-permute-start.3 = (bf16[2,1,48,256]{3,2,1,0:T(8,128)(2,1)S(1)}, bf16[2,1,48,256]{3,2,1,0:T(8,128)(2,1)S(1)}, u32[]{:S(2)}, u32[]{:S(2)}) collective-permute-start(bf16[2,1,48,256]{3,2,1,0:T(8,128)(2,1)S(1)} %get-tuple-element.42), channel_id=1, source_target_pairs={{16,0},{32,16},{48,32},{64,48},{80,64},{96,80},{112,96},{17,1},{33... | collective-permute-start | bytes 147464 | tf_op jit(solution)/shard_map/ppermute | solution.py:22
  16.5 11.3 %collective-permute-start = (bf16[2,1,48,256]{3,2,1,0:T(8,128)(2,1)S(1)}, bf16[2,1,48,256]{3,2,1,0:T(8,128)(2,1)S(1)}, u32[]{:S(2)}, u32[]{:S(2)}) collective-permute-start(bf16[2,1,48,256]{3,2,1,0:T(8,128)(2,1)S(1)} %get-tuple-element.42), channel_id=1, source_target_pairs={{0,8},{1,9},{2,10},{3,11},{4,12},{5,13},{6,14},{7,15},{8,0},{9,1},... | collective-permute-start | bytes 147464 | tf_op jit(solution)/shard_map/ppermute | solution.py:11
  17.1 1.4 copy-start.19
  17.3 9.9 %copy-start.15 = (f32[32]{0:T(128)}, f32[32]{0:T(128)S(1)}, u32[]{:S(2)}) copy-start(f32[32]{0:T(128)S(1)} %fusion.97) | copy-start | bytes 388
  27.1 1.4 copy-start
  27.8 5.9 %copy-start.12 = (bf16[2,1,48,256]{3,2,1,0:T(8,128)(2,1)}, bf16[2,1,48,256]{3,2,1,0:T(8,128)(2,1)S(1)}, u32[]{:S(2)}) copy-start(bf16[2,1,48,256]{3,2,1,0:T(8,128)(2,1)S(1)} %broadcast_select_fusion.1) | copy-start | bytes 147460
  28.5 5.2 %copy-start.14 = (bf16[2,1,48,256]{3,2,1,0:T(8,128)(2,1)}, bf16[2,1,48,256]{3,2,1,0:T(8,128)(2,1)S(1)}, u32[]{:S(2)}) copy-start(bf16[2,1,48,256]{3,2,1,0:T(8,128)(2,1)S(1)} %broadcast_select_fusion.3) | copy-start | bytes 147460
  28.6 3.3 %copy-start.8 = (bf16[9,256,256]{2,1,0:T(8,128)(2,1)S(1)}, bf16[9,256,256]{2,1,0:T(8,128)(2,1)}, u32[]{:S(2)}) copy-start(bf16[9,256,256]{2,1,0:T(8,128)(2,1)} %param.5) | copy-start | bytes 3538948
  28.8 4.8 %collective-permute-start.5 = (bf16[2,34,1,256]{3,2,1,0:T(2,128)(2,1)S(1)}, bf16[2,34,1,256]{3,2,1,0:T(2,128)(2,1)S(1)}, u32[]{:S(2)}, u32[]{:S(2)}) collective-permute-start(bf16[2,34,1,256]{3,2,1,0:T(2,128)(2,1)S(1)} %get-tuple-element.35), channel_id=1, source_target_pairs={{1,0},{2,1},{3,2},{4,3},{5,4},{6,5},{7,6},{8,7},{9,8},{10,9},{11,1... | collective-permute-start | bytes 104456 | tf_op jit(solution)/shard_map/ppermute | solution.py:22
  30.4 3.3 %collective-permute-start.4 = (bf16[2,34,1,256]{3,2,1,0:T(2,128)(2,1)S(1)}, bf16[2,34,1,256]{3,2,1,0:T(2,128)(2,1)S(1)}, u32[]{:S(2)}, u32[]{:S(2)}) collective-permute-start(bf16[2,34,1,256]{3,2,1,0:T(2,128)(2,1)S(1)} %get-tuple-element.36), channel_id=1, source_target_pairs={{0,1},{1,2},{2,3},{3,4},{4,5},{5,6},{6,7},{7,8},{8,9},{9,10},{10,1... | collective-permute-start | bytes 104456 | tf_op jit(solution)/shard_map/ppermute | solution.py:21
  34.9 3.1 %copy-start.2 = (bf16[2,34,49,256]{3,2,1,0:T(8,128)(2,1)}, bf16[2,34,49,256]{3,2,1,0:T(8,128)(2,1)S(1)}, u32[]{:S(2)}) copy-start(bf16[2,34,49,256]{3,2,1,0:T(8,128)(2,1)S(1)} %get-tuple-element.33) | copy-start | bytes 5117956
  41.5 1.9 copy-start.10
  41.5 1.9 copy-start.17
  43.4 2.2 copy-start.6
  43.4 2.2 copy-start.16
  45.6 1.7 copy-start.4
  48.0 106.5 %collective-permute-start.9 = (bf16[2,1,48,256]{3,2,1,0:T(8,128)(2,1)}, bf16[2,1,48,256]{3,2,1,0:T(8,128)(2,1)}, u32[]{:S(2)}, u32[]{:S(2)}) collective-permute-start(bf16[2,1,48,256]{3,2,1,0:T(8,128)(2,1)} %get-tuple-element.37), channel_id=1, source_target_pairs={{16,0},{32,16},{48,32},{64,48},{80,64},{96,80},{112,96},{17,1},{33... | collective-permute-start | bytes 147464 | tf_op jit(solution)/shard_map/ppermute | solution.py:22
  49.2 104.2 %collective-permute-start.6 = (bf16[2,1,48,256]{3,2,1,0:T(8,128)(2,1)}, bf16[2,1,48,256]{3,2,1,0:T(8,128)(2,1)}, u32[]{:S(2)}, u32[]{:S(2)}) collective-permute-start(bf16[2,1,48,256]{3,2,1,0:T(8,128)(2,1)} %get-tuple-element.37), channel_id=1, source_target_pairs={{0,8},{1,9},{2,10},{3,11},{4,12},{5,13},{6,14},{7,15},{8,0},{9,1},... | collective-permute-start | bytes 147464 | tf_op jit(solution)/shard_map/ppermute | solution.py:11
  52.1 102.4 %collective-permute-start.8 = (bf16[2,1,48,256]{3,2,1,0:T(8,128)(2,1)}, bf16[2,1,48,256]{3,2,1,0:T(8,128)(2,1)}, u32[]{:S(2)}, u32[]{:S(2)}) collective-permute-start(bf16[2,1,48,256]{3,2,1,0:T(8,128)(2,1)} %get-tuple-element.38), channel_id=1, source_target_pairs={{0,8},{1,9},{2,10},{3,11},{4,12},{5,13},{6,14},{7,15},{8,0},{9,1},... | collective-permute-start | bytes 147464 | tf_op jit(solution)/shard_map/ppermute | solution.py:11
  52.3 101.2 %collective-permute-start.7 = (bf16[2,1,48,256]{3,2,1,0:T(8,128)(2,1)}, bf16[2,1,48,256]{3,2,1,0:T(8,128)(2,1)}, u32[]{:S(2)}, u32[]{:S(2)}) collective-permute-start(bf16[2,1,48,256]{3,2,1,0:T(8,128)(2,1)} %get-tuple-element.38), channel_id=1, source_target_pairs={{0,16},{16,32},{32,48},{48,64},{64,80},{80,96},{96,112},{1,17},{17... | collective-permute-start | bytes 147464 | tf_op jit(solution)/shard_map/ppermute | solution.py:21
  64.2 2.9 %copy-start.3 = (bf16[2,34,49,256]{3,2,1,0:T(8,128)(2,1)S(1)}, bf16[2,34,49,256]{3,2,1,0:T(8,128)(2,1)}, u32[]{:S(2)}) copy-start(bf16[2,34,49,256]{3,2,1,0:T(8,128)(2,1)} %copy-done.2) | copy-start | bytes 5117956
  77.3 3.2 %copy-start.20 = (f32[16]{0:T(128)S(1)}, f32[16]{0:T(128)}, u32[]{:S(2)}) copy-start(f32[16]{0:T(128)} %copy-done.19) | copy-start | bytes 196
  77.3 4.1 %copy-start.21 = (f32[256]{0:T(256)S(1)}, f32[256]{0:T(256)}, u32[]{:S(2)}) copy-start(f32[256]{0:T(256)} %get-tuple-element.43) | copy-start | bytes 3076
  77.3 77.0 %copy-start.9 = (bf16[9,256,256]{2,1,0:T(8,128)(2,1)S(1)}, bf16[9,256,256]{2,1,0:T(8,128)(2,1)}, u32[]{:S(2)}) copy-start(bf16[9,256,256]{2,1,0:T(8,128)(2,1)} %param.5) | copy-start | bytes 3538948
  155.4 4.1 %collective-permute-start.11 = (bf16[2,34,1,256]{3,2,1,0:T(2,128)(2,1)S(1)}, bf16[2,34,1,256]{3,2,1,0:T(2,128)(2,1)S(1)}, u32[]{:S(2)}, u32[]{:S(2)}) collective-permute-start(bf16[2,34,1,256]{3,2,1,0:T(2,128)(2,1)S(1)} %get-tuple-element.31), channel_id=1, source_target_pairs={{1,0},{2,1},{3,2},{4,3},{5,4},{6,5},{7,6},{8,7},{9,8},{10,9},{11,1... | collective-permute-start | bytes 104456 | tf_op jit(solution)/shard_map/ppermute | solution.py:22
  156.3 3.3 %collective-permute-start.10 = (bf16[2,34,1,256]{3,2,1,0:T(2,128)(2,1)S(1)}, bf16[2,34,1,256]{3,2,1,0:T(2,128)(2,1)S(1)}, u32[]{:S(2)}, u32[]{:S(2)}) collective-permute-start(bf16[2,34,1,256]{3,2,1,0:T(2,128)(2,1)S(1)} %get-tuple-element.32), channel_id=1, source_target_pairs={{0,1},{1,2},{2,3},{3,4},{4,5},{5,6},{6,7},{7,8},{8,9},{9,10},{10,1... | collective-permute-start | bytes 104456 | tf_op jit(solution)/shard_map/ppermute | solution.py:21
  162.2 1.5 slice-start
  167.6 1.9 copy-start.5
  167.6 2.8 %copy-start.11 = (f32[3072,256]{1,0:T(8,128)S(1)}, f32[3072,256]{1,0:T(8,128)}, u32[]{:S(2)}) copy-start(f32[3072,256]{1,0:T(8,128)} %reshape.184) | copy-start | bytes 9437188
  (4 other events, 4.7 us)
Sparse Core Ops, SparseCore 0:
  76.7 157.3 all-reduce.1
where the time goes:
time: 245 us; the launch traced here: 244 us
  blocking collectives  72.1 us (29%)
  waiting for transfers between devices  60.1 us (25%)
  local copies, waits for them, and re-layouts  30.9 us (13%)
  matrix products  27.7 us (11%)
  starting transfers between devices  24.1 us (10%)
  other arithmetic  14.8 us (6%)
  between operations  14.5 us (6%)
    psum x1, blocking collectives, local(): grad_kernel, grad_bias = lax.psum((kernel_part, bias_part), ('lat', 'lon'))  72.1 us
    psum x1, waiting for transfers between devices, local(): grad_kernel, grad_bias = lax.psum((kernel_part, bias_part), ('lat', 'lon'))  57.3 us
    dot_general x9, matrix products, kernel_grad(): lax.dot_general(window, flat_grad, (((0,), (0,)), ((), ())), preferred_el...  13.5 us
    ppermute x4, starting transfers between devices, with_halo(): before = lax.ppermute(last, axis, up)  12 us
    unnamed x45, local copies, waits for them, and re-layouts  8.65 us
    ppermute x4, starting transfers between devices, shifted(): lax.ppermute(shard, axis, [(i, (i + by) % size) for i in range(size)])  6.98 us
    reshape x2, local copies, waits for them, and re-layouts, local(): jnp.repeat(jnp.repeat(cotangent.astype(jnp.float32), 2, axis=1), 2, axis=2)  6.82 us
    dot_general x9, matrix products, forward_conv(): jnp.dot(window, kernel[3 * row_off + col_off], preferred_element_type=jnp...  6.79 us
  transfers between devices with their start and end apart: 13, of which 4 were waited for; matrix products, arithmetic and copies ran while one was open for 21% of the time, Pallas kernels for 0%

commit v1 on v0

v1 whole, which is shorter than its diff:
```python
import math

import jax
import jax.numpy as jnp
from jax import lax
from jax.experimental import pallas as pl
from jax.experimental.pallas import tpu as pltpu
from jax.sharding import Mesh, PartitionSpec as P

F32 = jnp.float32
BF16 = jnp.bfloat16
LAT = ("yh", "z")
LON = ("x", "yl", "core")
RING = ("yh", "yl")
PLANE = ("x", "z")


def edge_block(right0, right1, left0, left1, chans):
    place = lax.broadcasted_iota(jnp.int32, (8, chans), 0)
    return jnp.where(
        place == 0,
        right0,
        jnp.where(place == 1, right1, jnp.where(place == 6, left0, jnp.where(place == 7, left1, 0.0))),
    )


def forward_kernel(
    flags, share, field, from_fore, from_aft, from_right, from_left, cot, weights, bias,
    pooled, grad, keep, give, wide, right, left, spread, pool, flipped, total, bias_total,
):
    batches, rows, cols, chans = field.shape
    width = cols + 8
    pairs = rows // 2
    step = 8
    is_north, is_south, first_half, core = flags[0], flags[1], flags[2], flags[3]
    right[...] = from_right[...].astype(F32)
    left[...] = from_left[...].astype(F32)
    span = rows + 4

    def put(b, e, own):
        edge = edge_block(
            right[b, pl.ds(e, 1), :], right[b, pl.ds(span + e, 1), :],
            left[b, pl.ds(e, 1), :], left[b, pl.ds(span + e, 1), :], chans,
        )
        line = jnp.concatenate([own, edge], axis=0)
        wide[b, e, :, :chans] = pltpu.roll(line, 1, 0).astype(BF16)
        wide[b, e, :, chans : 2 * chans] = line.astype(BF16)
        wide[b, e, :, 2 * chans :] = pltpu.roll(line, width - 1, 0).astype(BF16)

    def halo(b, lo, hi):
        fore = from_fore[b, lo:hi, :].astype(F32)
        aft = from_aft[b, lo:hi, :].astype(F32)
        top = jnp.where(first_half == 1, fore, aft)
        bottom = jnp.where(first_half == 1, aft, fore)
        return top, bottom

    for b in range(batches):
        for k in range(2):
            top, bottom = halo(b, k * cols, (k + 1) * cols)
            put(b, k, top)
            put(b, rows + 2 + k, bottom)

        def fill(i, carry):
            put(b, i + 2, field[b, i].astype(F32))
            return carry

        lax.fori_loop(0, rows, fill, 0, unroll=4)

    def conv(parts):
        acc = None
        for r in range(3):
            term = jnp.dot(parts[r], weights[r], preferred_element_type=F32)
            acc = term if acc is None else acc + term
        return acc + bias[...]

    def slope(pre):
        sigma = 1.0 / (1.0 + jnp.exp(-pre))
        return sigma, sigma * (1.0 + pre * (1.0 - sigma))

    def join(ref, slot, at):
        return jnp.concatenate([ref[slot, h, at, :] for h in range(chans // 128)], axis=-1)

    def lift(slot, b, q, own):
        for h in range(chans // 128):
            for k in range(2):
                spread[slot, h, pl.ds(k, cols // 2, stride=2), :] = own[:, h * 128 : h * 128 + 128]
        place = lax.broadcasted_iota(jnp.int32, (8, chans), 0)
        edge = jnp.where(
            place == 0,
            right[b, pl.ds(2 * span + q, 1), :],
            jnp.where(place == 7, left[b, pl.ds(2 * span + q, 1), :], 0.0),
        )
        return jnp.concatenate([join(spread, slot, slice(0, cols)), edge], axis=0)

    for t in range(2):
        base = 0 if t == 0 else rows + 1
        turned = is_north if t == 0 else is_south
        parts = []
        for r in range(3):
            at = base + jnp.where(turned == 1, 2 - r, r)
            parts.append(wide[:, pl.ds(at, 1), :, :].reshape(batches * width, 3 * chans))
        _, rate = slope(conv(parts))
        for b in range(batches):
            cot_rows = halo(b, 2 * cols, 2 * cols + cols // 2)[t]
            value = lift(0, b, 0 if t == 0 else pairs + 1, cot_rows) * share[0 if t == 0 else rows + 1] * rate[b * width : (b + 1) * width]
            grad[b, 0 if t == 0 else rows + 1] = value.astype(BF16)

    bias_total[...] = jnp.zeros_like(bias_total)
    blocks = rows // step

    def block(n, carry):
        b = n // blocks
        first = (n % blocks) * step
        parts = [
            wide[b, pl.ds(first + 1 + r, step), :, :].reshape(step * width, 3 * chans) for r in range(3)
        ]
        pre = conv(parts)
        sigma, rate = slope(pre)
        active = (pre * sigma).astype(BF16).astype(F32).reshape(step, width, chans)
        rate = rate.reshape(step, width, chans)
        lines = []
        for m in range(step // 2):
            q = first // 2 + m
            up, low = share[first + 2 * m + 1], share[first + 2 * m + 2]
            mixed = (active[2 * m] * up + active[2 * m + 1] * low)[:cols]
            for h in range(chans // 128):
                pool[m, h] = mixed[:, h * 128 : h * 128 + 128]
            even, odd = (join(pool, m, pl.ds(k, cols // 2, stride=2)) for k in range(2))
            pooled[b, q] = (even + odd).astype(BF16)
            lifted = lift(m, b, q + 1, cot[b, q].astype(F32))
            for k, part in ((2 * m, up), (2 * m + 1, low)):
                value = (lifted * part * rate[k]).astype(BF16)
                grad[b, first + k + 1] = value
                lines.append(value[:cols])
        own = jnp.concatenate(lines, axis=0)
        bias_total[...] += own.astype(F32).reshape(-1, 8, chans).sum(axis=0)
        at = pl.multiple_of(n * (step * cols), 128)
        flipped[:, pl.ds(at, step * cols)] = own.T
        return carry

    lax.fori_loop(0, batches * blocks, block, 0)

    size = rows * cols
    for r in range(3):
        acc = None
        for b in range(batches):
            term = jnp.dot(
                flipped[:, b * size : (b + 1) * size],
                wide[b, 1 + r : 1 + r + rows, :cols, :].reshape(size, 3 * chans),
                preferred_element_type=F32,
            )
            acc = term if acc is None else acc + term
        total[r * 3 * chans : (r + 1) * 3 * chans, :] = acc.T
    bias_sum = bias_total[...].sum(axis=0, keepdims=True)
    place = lax.broadcasted_iota(jnp.int32, (8, chans), 0)
    parts_count, deep = keep.shape[0], keep.shape[1] - 8
    for ref, side in ((keep, core), (give, 1 - core)):
        for j in range(parts_count):
            at = pl.multiple_of((side * parts_count + j) * deep, 8)
            ref[j, :deep, :] = total[pl.ds(at, deep), :].astype(ref.dtype)
            tail = jnp.where((place == 0) & (side == 0), bias_sum, 0.0) if j == 0 else jnp.zeros((8, chans), F32)
            ref[j, deep:, :] = tail.astype(ref.dtype)


def back_kernel(flags, grad, weights, out, wide, ends, acc):
    batches, slots, width, chans = grad.shape
    rows, cols = slots - 2, width - 8
    step = 8
    is_north, is_south = flags[0], flags[1]

    def put(line, ref, index):
        line = line.astype(F32)
        ref[(*index, slice(None), slice(0, chans))] = pltpu.roll(line, 1, 0)[:cols].astype(BF16)
        ref[(*index, slice(None), slice(chans, 2 * chans))] = line[:cols].astype(BF16)
        ref[(*index, slice(None), slice(2 * chans, 3 * chans))] = pltpu.roll(line, width - 1, 0)[:cols].astype(BF16)

    for b in range(batches):
        put(grad[b, 0], ends, (0, b))
        put(grad[b, slots - 1], ends, (1, b))
        wide[b, 0] = jnp.zeros_like(wide[b, 0])
        wide[b, slots - 1] = jnp.zeros_like(wide[b, slots - 1])

        def fill(i, carry):
            put(grad[b, i + 1], wide, (b, i + 1))
            return carry

        lax.fori_loop(0, rows, fill, 0, unroll=4)

    for t in range(2):
        tap = jnp.where(is_north == 1, 0, 2) if t == 0 else jnp.where(is_south == 1, 2, 0)
        lines = ends[t].reshape(batches * cols, 3 * chans)
        acc[t] = jnp.dot(lines, weights[tap], preferred_element_type=F32).reshape(batches, cols, chans)

    for b in range(batches):
        for first in range(0, rows, step):
            total = None
            for r in range(3):
                lines = wide[b, first + 2 - r : first + 2 - r + step, :, :].reshape(step * cols, 3 * chans)
                term = jnp.dot(lines, weights[r], preferred_element_type=F32)
                total = term if total is None else total + term
            total = total.reshape(step, cols, chans)
            for k in range(step):
                line = total[k]
                if first + k == 0:
                    line = line + acc[0, b]
                if first + k == rows - 1:
                    line = line + acc[1, b]
                out[b, first + k] = line.astype(BF16)


def circle(lats, lons):
    half = lons // 2
    fore = []
    for a in range(lats):
        for l in range(lons):
            if l < half:
                to = (a + 1, l) if a < lats - 1 else (a, l + half)
            else:
                to = (a - 1, l) if a > 0 else (a, l - half)
            fore.append((a * lons + l, to[0] * lons + to[1]))
    return fore, [(j, i) for i, j in fore]


def row_pair(field, at0, at1):
    return jnp.concatenate(
        [lax.dynamic_slice_in_dim(field, at0, 1, 1), lax.dynamic_slice_in_dim(field, at1, 1, 1)], axis=1
    )


def vmem():
    return pl.BlockSpec(memory_space=pltpu.VMEM)


def local(fields, kernel, conv_bias, cotangent):
    batches, rows, cols, chans = fields.shape
    lat_count, lon_count = lax.axis_size(LAT), lax.axis_size(LON)
    lat, lon = lax.axis_index(LAT), lax.axis_index(LON)
    first_half = lon < lon_count // 2
    is_north, is_south = lat == 0, lat == lat_count - 1
    pairs, halves = rows // 2, cols // 2

    low = (jnp.where(is_south, rows - 1, rows - 2), jnp.where(is_south, rows - 2, rows - 1), pairs - 1)
    high = (jnp.where(is_north, 1, 0), jnp.where(is_north, 0, 1), 0)

    def message(down):
        at = [jnp.where(down, x, y) for x, y in zip(low, high)]
        return jnp.concatenate(
            [
                row_pair(fields, at[0], at[1]).reshape(batches, 2 * cols, chans),
                lax.dynamic_slice_in_dim(cotangent, at[2], 1, 1).reshape(batches, halves, chans),
            ],
            axis=1,
        )

    fore, aft = circle(lat_count, lon_count)
    from_fore = lax.ppermute(message(first_half), LAT + LON, fore)
    from_aft = lax.ppermute(message(~first_half), LAT + LON, aft)
    top = jnp.where(first_half, from_fore, from_aft)
    bottom = jnp.where(first_half, from_aft, from_fore)

    def column(c):
        return [
            top[:, c : c + 1], top[:, cols + c : cols + c + 1], fields[:, :, c],
            bottom[:, c : c + 1], bottom[:, cols + c : cols + c + 1],
        ]

    def cot_column(c):
        at = 2 * cols + c
        return [top[:, at : at + 1], cotangent[:, :, c], bottom[:, at : at + 1]]

    to_left = jnp.concatenate(column(0) + column(1) + cot_column(0), axis=1)
    to_right = jnp.concatenate(column(cols - 2) + column(cols - 1) + cot_column(halves - 1), axis=1)
    ring = [(i, (i + 1) % lon_count) for i in range(lon_count)]
    from_left = lax.ppermute(to_right, LON, ring)
    from_right = lax.ppermute(to_left, LON, [(j, i) for i, j in ring])

    total_rows = rows * lat_count
    index = jnp.clip(lat * rows - 1 + jnp.arange(rows + 2), 0, total_rows - 1)

    def cosine(at):
        return jnp.cos((at.astype(F32) + 0.5) * (math.pi / total_rows) - math.pi / 2)

    even = index // 2 * 2
    share = cosine(index) / (2.0 * (cosine(even) + cosine(even + 1)))
    core = lax.axis_index("core")
    flags = jnp.stack([is_north, is_south, first_half, core == 1]).astype(jnp.int32)

    weights = kernel.reshape(3, 3 * chans, chans)
    back_weights = jnp.swapaxes(kernel.reshape(3, 3, chans, chans)[:, ::-1], 2, 3).reshape(3, 3 * chans, chans)
    plane = lax.axis_size(PLANE)
    deep = 9 * chans // (2 * plane)
    smem = pl.BlockSpec(memory_space=pltpu.SMEM)
    message_type = jax.ShapeDtypeStruct((plane, deep + 8, chans), BF16)
    count = from_right.shape[1]
    pooled, grad, keep, give = pl.pallas_call(
        forward_kernel,
        out_shape=(
            jax.ShapeDtypeStruct((batches, pairs, halves, chans), BF16),
            jax.ShapeDtypeStruct((batches, rows + 2, cols + 8, chans), BF16),
            message_type,
            message_type,
        ),
        in_specs=[smem, smem] + [vmem()] * 8,
        out_specs=[vmem()] * 4,
        scratch_shapes=[
            pltpu.VMEM((batches, rows + 4, cols + 8, 3 * chans), BF16),
            pltpu.VMEM((batches, count, chans), F32),
            pltpu.VMEM((batches, count, chans), F32),
            pltpu.VMEM((4, chans // 128, cols, 128), F32),
            pltpu.VMEM((4, chans // 128, cols, 128), F32),
            pltpu.VMEM((chans, batches * rows * cols), BF16),
            pltpu.VMEM((9 * chans, chans), F32),
            pltpu.VMEM((8, chans), F32),
        ],
        name="forward",
    )(flags, share, fields, from_fore, from_aft, from_right, from_left, cotangent, weights, conv_bias[None])

    back = pl.pallas_call(
        back_kernel,
        out_shape=jax.ShapeDtypeStruct((batches, rows, cols, chans), BF16),
        in_specs=[smem, vmem(), vmem()],
        out_specs=vmem(),
        scratch_shapes=[
            pltpu.VMEM((batches, rows + 2, cols, 3 * chans), BF16),
            pltpu.VMEM((2, batches, cols, 3 * chans), BF16),
            pltpu.VMEM((2, batches, cols, chans), F32),
        ],
        name="back",
    )(flags, grad, back_weights)

    take = lax.ppermute(give, "core", [(0, 1), (1, 0)])
    part = (keep.astype(F32) + take.astype(F32)).astype(BF16)
    part = lax.all_to_all(part, PLANE, 0, 0, tiled=True)
    part = part.astype(F32).sum(axis=0).astype(BF16)
    size = lax.axis_size(RING)
    total = part.astype(F32)
    for k in range(1, size):
        total = total + lax.ppermute(part, RING, [(i, (i + k) % size) for i in range(size)]).astype(F32)
    total = jnp.broadcast_to(total.astype(BF16)[None], (plane, deep + 8, chans))
    total = lax.all_to_all(total, PLANE, 0, 0, tiled=True)
    total = lax.all_gather(total, "core", axis=0, tiled=True)
    grad_kernel = total[:, :deep].astype(F32).reshape(9, chans, chans)
    grad_bias = total[0, deep].astype(F32)
    return pooled, back, grad_kernel, grad_bias


def solution(mesh):
    lats, lons = mesh.devices.shape
    fine = Mesh(mesh.devices.reshape(2, lats // 2, lons // 4, 2, 2), LAT + LON)
    spec = P(None, LAT, LON, None)
    return jax.shard_map(
        local,
        mesh=fine,
        in_specs=(spec, P(), P(), spec),
        out_specs=(spec, spec, P(), P()),
        check_vma=False,
    )
```

time: 245 us -> 110 us (0.45)
  waiting for transfers between devices: 60.1 us -> 11 us
  blocking collectives: 72.1 us -> 32.6 us
  matrix products: 27.7 us -> 0 us
  Pallas kernels: 0 us -> 24.3 us
  local copies, waits for them, and re-layouts: 30.9 us -> 9.29 us
  starting transfers between devices: 24.1 us -> 13 us
  other arithmetic: 14.8 us -> 4.84 us
    psum x1 -> x0, blocking collectives: 72.1 us -> none  [local(): grad_kernel, grad_bias = lax.psum((kernel_part, bias_part), ('lat', 'lon'))]
    psum x1 -> x0, waiting for transfers between devices: 57.3 us -> none  [local(): grad_kernel, grad_bias = lax.psum((kernel_part, bias_part), ('lat', 'lon'))]
    all_to_all x0 -> x2, blocking collectives: none -> 32.6 us  [the longest x1 19 us: local(): part = lax.all_to_all(part, PLANE, 0, 0, tiled=True)]
    dot_general x33 -> x0, matrix products: 27.7 us -> none  [the longest x9 13.5 us: kernel_grad(): lax.dot_general(window, flat_grad, (((0,), (0,)), ((), ())), preferred_el...]
    pallas_call x0 -> x2, Pallas kernels: none -> 24.3 us  [the longest x1 16.5 us: local(): pl.pallas_call(forward_kernel, out_shape=(jax.ShapeDtypeStruct((batches,...]
    ppermute x12 -> x8, starting transfers between devices: 24 us -> 12.9 us  [the longest x1 3.63 us: local(): from_aft = lax.ppermute(message(~first_half), LAT + LON, aft)]
    reshape x3 -> x2, local copies, waits for them, and re-layouts: 12 us -> 1.5 us  [the longest x1 0.77 us: message(): lax.dynamic_slice_in_dim(cotangent, at[2], 1, 1)]
    unnamed x45 -> x14, local copies, waits for them, and re-layouts: 8.65 us -> 0.77 us
  transfers between devices with their start and end apart: 13 -> 9, of which waited for: 4 -> 7; matrix products, arithmetic and copies ran while one was open for 21% -> 6% of each run, Pallas kernels for 0% -> 7%
where the time goes in v1:
time: 110 us; the launch traced here: 109 us
  blocking collectives  32.6 us (30%)
  Pallas kernels  24.3 us (22%)
  between operations  14.2 us (13%)
  starting transfers between devices  13 us (12%)
  waiting for transfers between devices  11 us (10%)
  local copies, waits for them, and re-layouts  9.29 us (8%)
  other arithmetic  4.84 us (4%)
    all_to_all x1, blocking collectives, local(): part = lax.all_to_all(part, PLANE, 0, 0, tiled=True)  19 us
    pallas_call x1, Pallas kernels, local(): pl.pallas_call(forward_kernel, out_shape=(jax.ShapeDtypeStruct((batches,...  16.5 us
    all_to_all x1, blocking collectives, local(): total = lax.all_to_all(total, PLANE, 0, 0, tiled=True)  13.6 us
    pallas_call x1, Pallas kernels, local(): pl.pallas_call(back_kernel, out_shape=jax.ShapeDtypeStruct((batches, rows...  7.72 us
    ppermute x3, waiting for transfers between devices, local(): lax.ppermute(part, RING, [(i, (i + k) % size) for i in range(size)])  3.9 us
    ppermute x1, starting transfers between devices, local(): from_aft = lax.ppermute(message(~first_half), LAT + LON, aft)  3.63 us
    ppermute x1, starting transfers between devices, local(): take = lax.ppermute(give, 'core', [(0, 1), (1, 0)])  3.28 us
    ppermute x3, starting transfers between devices, local(): lax.ppermute(part, RING, [(i, (i + k) % size) for i in range(size)])  2.5 us
  transfers between devices with their start and end apart: 9, of which 7 were waited for; matrix products, arithmetic and copies ran while one was open for 6% of the time, Pallas kernels for 7%

profile of v1, /device:TPU:1, one launch (start us, length us, event | category | flops | bytes accessed | tf_op | source)
XLA Modules:
  0.0 109.2 jit_solution(5325169114289951073)
XLA Ops:
  7.3 0.8 dynamic-slice_bitcast_fusion
  8.0 0.9 constant_dynamic-slice_fusion.1
  9.0 3.6 %collective-permute-start.1 = (bf16[2,120,256]{2,1,0:T(8,128)(2,1)S(1)}, bf16[2,120,256]{2,1,0:T(8,128)(2,1)S(1)}, u32[]{:S(2)}, u32[]{:S(2)}) collective-permute-start(bf16[2,120,256]{2,1,0:T(8,128)(2,1)S(1)} %pad_maximum_fusion.1), channel_id=1, source_target_pairs={{16,0},{17,1},{18,2},{19,3},{20,4},{21,5},{22,6},{23,7},{0,8},{1,9... | collective-permute-start | bytes 368648 | tf_op jit(solution)/shard_map/ppermute | solution.py:257
  12.7 1.0 fusion.1
  13.7 1.6 %fusion = (bf16[2,32,1,256]{3,2,1,0:T(2,128)(2,1)S(1)}, bf16[2,32,1,256]{3,2,1,0:T(2,128)(2,1)S(1)}, bf16[2,32,1,256]{3,2,1,0:T(2,128)(2,1)S(1)}, bf16[2,32,1,256]{3,2,1,0:T(2,128)(2,1)S(1)}) fusion(bf16[2,32,48,256]{3,2,1,0:T(8,128)(2,1)} %field.1), kind=kLoop, calls=%fused_computation.27 | loop fusion | bytes 262144 | tf_op jit(solution)/shard_map/slice | solution.py:263
  15.3 0.6 multiply_divide_fusion.share
  16.0 1.9 %collective-permute-done.from_fore = bf16[2,120,256]{2,1,0:T(8,128)(2,1)S(1)} collective-permute-done((bf16[2,120,256]{2,1,0:T(8,128)(2,1)S(1)}, bf16[2,120,256]{2,1,0:T(8,128)(2,1)S(1)}, u32[]{:S(2)}, u32[]{:S(2)}) %collective-permute-start) | collective-permute-done | bytes 122912 | tf_op jit(solution)/shard_map/ppermute | solution.py:256
  18.0 0.5 concatenate.22
  18.5 2.2 %collective-permute-start.2 = (bf16[2,90,256]{2,1,0:T(8,128)(2,1)S(1)}, bf16[2,90,256]{2,1,0:T(8,128)(2,1)S(1)}, u32[]{:S(2)}, u32[]{:S(2)}) collective-permute-start(bf16[2,90,256]{2,1,0:T(8,128)(2,1)S(1)} %concatenate.22), channel_id=1, source_target_pairs={{1,0},{2,1},{3,2},{4,3},{5,4},{6,5},{7,6},{8,7},{9,8},{10,9},{11,1... | collective-permute-start | bytes 276488 | tf_op jit(solution)/shard_map/ppermute | solution.py:275
  20.7 0.5 concatenate.23
  21.2 1.3 %collective-permute-start.3 = (bf16[2,90,256]{2,1,0:T(8,128)(2,1)S(1)}, bf16[2,90,256]{2,1,0:T(8,128)(2,1)S(1)}, u32[]{:S(2)}, u32[]{:S(2)}) collective-permute-start(bf16[2,90,256]{2,1,0:T(8,128)(2,1)S(1)} %concatenate.23), channel_id=1, source_target_pairs={{0,1},{1,2},{2,3},{3,4},{4,5},{5,6},{6,7},{7,8},{8,9},{9,10},{10,1... | collective-permute-start | bytes 276488 | tf_op jit(solution)/shard_map/ppermute | solution.py:274
  22.5 0.6 add_convert_fusion.2.flags
  23.1 1.1 collective-permute-done.2.from_right
  24.2 0.6 copy-done.4
  24.9 16.5 %forward.1 = (bf16[2,16,24,256]{3,2,1,0:T(8,128)(2,1)}, bf16[2,34,56,256]{3,2,1,0:T(8,128)(2,1)}, bf16[16,80,256]{2,1,0:T(8,128)(2,1)}, bf16[16,80,256]{2,1,0:T(8,128)(2,1)}) custom-call(s32[4]{0:T(128)} %add_convert_fusion.2.flags, f32[34]{0:T(128)} %multiply_divide_fusion.share, bf16[2,32,48,256]{3,2,1,0:T(8,128)(2,1)} %field.1, ...), custom_call_target="tpu_custom_call" | custom-call | tf_op jit(solution)/shard_map/forward/pallas_call | solution.py:295
  41.4 3.3 %collective-permute-start.4 = (bf16[16,80,256]{2,1,0:T(8,128)(2,1)}, bf16[16,80,256]{2,1,0:T(8,128)(2,1)S(1)}, u32[]{:S(2)}, u32[]{:S(2)}) collective-permute-start(bf16[16,80,256]{2,1,0:T(8,128)(2,1)} %get-tuple-element.11), channel_id=1, source_target_pairs={{0,1},{1,0},{2,3},{3,2},{4,5},{5,4},{6,7},{7,6},{8,9},{9,8},{10,11... | collective-permute-start | bytes 1966088 | tf_op jit(solution)/shard_map/ppermute | solution.py:331
  44.7 1.9 %collective-permute-done.4 = bf16[16,80,256]{2,1,0:T(8,128)(2,1)S(1)} collective-permute-done((bf16[16,80,256]{2,1,0:T(8,128)(2,1)}, bf16[16,80,256]{2,1,0:T(8,128)(2,1)S(1)}, u32[]{:S(2)}, u32[]{:S(2)}) %collective-permute-start.4) | collective-permute-done | bytes 655392 | tf_op jit(solution)/shard_map/ppermute | solution.py:331
  46.6 1.3 %add_convert_fusion = bf16[16,80,256]{2,1,0:T(8,128)(2,1)S(1)} fusion(bf16[16,80,256]{2,1,0:T(8,128)(2,1)S(1)} %collective-permute-done.4, bf16[16,80,256]{2,1,0:T(8,128)(2,1)} %get-tuple-element.10), kind=kLoop, calls=%fused_computation | loop fusion | flops 1310720 | bytes 1966080 | tf_op jit(solution)/shard_map/convert_element_type | solution.py:332
  47.9 19.0 %all_to_all.10 = bf16[16,80,256]{2,1,0:T(8,128)(2,1)S(1)} all-to-all(bf16[16,80,256]{2,1,0:T(8,128)(2,1)S(1)} %add_convert_fusion), channel_id=1, replica_groups=mesh['yh'=2,'z'=4,'x'=4,'yl'=2,'core'=2] {'x','z'}, dimensions={0} | all-to-all | bytes 1310720 | tf_op jit(solution)/shard_map/all_to_all | solution.py:333
  67.2 2.2 %collective-permute-start.6 = (bf16[80,256]{1,0:T(8,128)(2,1)S(1)}, bf16[80,256]{1,0:T(8,128)(2,1)S(1)}, u32[]{:S(2)}, u32[]{:S(2)}) collective-permute-start(bf16[80,256]{1,0:T(8,128)(2,1)S(1)} %reduce_sum.12), channel_id=1, source_target_pairs={{0,64},{2,66},{64,0},{66,2},{1,65},{3,67},{65,1},{67,3},{4,68},{6,... | collective-permute-start | bytes 122888 | tf_op jit(solution)/shard_map/ppermute | solution.py:338
  69.4 0.2 collective-permute-start.5
  69.5 0.4 collective-permute-done.7
  69.9 1.6 %collective-permute-done.6 = bf16[80,256]{1,0:T(8,128)(2,1)S(1)} collective-permute-done((bf16[80,256]{1,0:T(8,128)(2,1)S(1)}, bf16[80,256]{1,0:T(8,128)(2,1)S(1)}, u32[]{:S(2)}, u32[]{:S(2)}) %collective-permute-start.6) | collective-permute-done | bytes 40992 | tf_op jit(solution)/shard_map/ppermute | solution.py:338
  71.5 1.9 %collective-permute-done.5 = bf16[80,256]{1,0:T(8,128)(2,1)S(1)} collective-permute-done((bf16[80,256]{1,0:T(8,128)(2,1)S(1)}, bf16[80,256]{1,0:T(8,128)(2,1)S(1)}, u32[]{:S(2)}, u32[]{:S(2)}) %collective-permute-start.5) | collective-permute-done | bytes 40992 | tf_op jit(solution)/shard_map/ppermute | solution.py:338
  73.5 13.6 %all_to_all.11 = bf16[16,80,256]{2,1,0:T(8,128)(2,1)} all-to-all(bf16[16,80,256]{2,1,0:T(8,128)(2,1)S(1)} %broadcast_in_dim.10), channel_id=1, replica_groups=mesh['yh'=2,'z'=4,'x'=4,'yl'=2,'core'=2] {'x','z'}, dimensions={0} | all-to-all | bytes 1310720 | tf_op jit(solution)/shard_map/all_to_all | solution.py:340
  87.1 0.7 copy.21
  87.9 1.1 %rev.3 = bf16[3,3,256,256]{2,3,1,0:T(8,128)(2,1)} reverse(bf16[3,3,256,256]{2,3,1,0:T(8,128)(2,1)S(1)} %copy.21), dimensions={1} | reverse | bytes 2359296 | tf_op jit(solution)/shard_map/rev | solution.py:289
  89.0 7.7 %back.1 = bf16[2,32,48,256]{3,2,1,0:T(8,128)(2,1)} custom-call(s32[4]{0:T(128)} %add_convert_fusion.2.flags, bf16[2,34,56,256]{3,2,1,0:T(8,128)(2,1)} %get-tuple-element.9.grad, bf16[3,768,256]{2,1,0:T(8,128)(2,1)} %bitcast.35), custom_call_target="tpu_custom_call" | custom-call | tf_op jit(solution)/shard_map/back/pallas_call | solution.py:318
  96.7 2.2 %all-gather.2.cloned.1.call-done = bf16[32,80,256]{2,1,0:T(8,128)(2,1)} async-done(((bf16[16,80,256]{2,1,0:T(8,128)(2,1)}), bf16[32,80,256]{2,1,0:T(8,128)(2,1)}) %all-gather.2.cloned.1.call-update) | async-done | bytes 1310736 | tf_op jit(solution)/shard_map/all_gather | solution.py:341
  98.8 1.3 %slice-done = bf16[32,72,256]{2,1,0:T(8,128)(2,1)S(1)} async-done(((bf16[32,80,256]{2,1,0:T(8,128)(2,1)}), bf16[32,72,256]{2,1,0:T(8,128)(2,1)S(1)}, s32[]{:S(2)}) %slice-start) | async-done | bytes 1179672 | tf_op jit(solution)/shard_map/slice | solution.py:342
  100.1 1.6 %convert.3 = f32[9,256,256]{2,1,0:T(8,128)} convert(bf16[9,256,256]{2,1,0:T(8,128)(2,1)S(1)} %bitcast.36) | non-fusion elementwise | flops 589824 | bytes 3538944 | tf_op jit(solution)/shard_map/reshape | solution.py:342
  101.8 0.6 slice_convert_fusion
  (31 shorter events, 0.7 us)
Async XLA Ops:
  7.2 91.7 %all-gather.2.cloned.1.call-start = ((), (), s32[]{:S(2)}) async-start(), calls=%async_computation.2 | async-start | bytes 1966080 | tf_op jit(solution)/shard_map/all_gather | solution.py:341
  9.0 7.0 %collective-permute-start.1 = (bf16[2,120,256]{2,1,0:T(8,128)(2,1)S(1)}, bf16[2,120,256]{2,1,0:T(8,128)(2,1)S(1)}, u32[]{:S(2)}, u32[]{:S(2)}) collective-permute-start(bf16[2,120,256]{2,1,0:T(8,128)(2,1)S(1)} %pad_maximum_fusion.1), channel_id=1, source_target_pairs={{16,0},{17,1},{18,2},{19,3},{20,4},{21,5},{22,6},{23,7},{0,8},{1,9... | collective-permute-start | bytes 368648 | tf_op jit(solution)/shard_map/ppermute | solution.py:257
  12.6 5.3 %collective-permute-start = (bf16[2,120,256]{2,1,0:T(8,128)(2,1)S(1)}, bf16[2,120,256]{2,1,0:T(8,128)(2,1)S(1)}, u32[]{:S(2)}, u32[]{:S(2)}) collective-permute-start(bf16[2,120,256]{2,1,0:T(8,128)(2,1)S(1)} %pad_maximum_fusion), channel_id=1, source_target_pairs={{0,16},{1,17},{2,18},{3,19},{4,20},{5,21},{6,22},{7,23},{8,0},{9,1... | collective-permute-start | bytes 368648 | tf_op jit(solution)/shard_map/ppermute | solution.py:256
  16.0 8.2 %copy-start.2 = (bf16[2,120,256]{2,1,0:T(8,128)(2,1)}, bf16[2,120,256]{2,1,0:T(8,128)(2,1)S(1)}, u32[]{:S(2)}) copy-start(bf16[2,120,256]{2,1,0:T(8,128)(2,1)S(1)} %collective-permute-done.1.from_aft) | copy-start | bytes 368644
  17.9 6.3 %copy-start.3 = (bf16[2,120,256]{2,1,0:T(8,128)(2,1)}, bf16[2,120,256]{2,1,0:T(8,128)(2,1)S(1)}, u32[]{:S(2)}) copy-start(bf16[2,120,256]{2,1,0:T(8,128)(2,1)S(1)} %collective-permute-done.from_fore) | copy-start | bytes 368644
  18.5 5.7 %collective-permute-start.2 = (bf16[2,90,256]{2,1,0:T(8,128)(2,1)S(1)}, bf16[2,90,256]{2,1,0:T(8,128)(2,1)S(1)}, u32[]{:S(2)}, u32[]{:S(2)}) collective-permute-start(bf16[2,90,256]{2,1,0:T(8,128)(2,1)S(1)} %concatenate.22), channel_id=1, source_target_pairs={{1,0},{2,1},{3,2},{4,3},{5,4},{6,5},{7,6},{8,7},{9,8},{10,9},{11,1... | collective-permute-start | bytes 276488 | tf_op jit(solution)/shard_map/ppermute | solution.py:275
  21.2 3.0 %collective-permute-start.3 = (bf16[2,90,256]{2,1,0:T(8,128)(2,1)S(1)}, bf16[2,90,256]{2,1,0:T(8,128)(2,1)S(1)}, u32[]{:S(2)}, u32[]{:S(2)}) collective-permute-start(bf16[2,90,256]{2,1,0:T(8,128)(2,1)S(1)} %concatenate.23), channel_id=1, source_target_pairs={{0,1},{1,2},{2,3},{3,4},{4,5},{5,6},{6,7},{7,8},{8,9},{9,10},{10,1... | collective-permute-start | bytes 276488 | tf_op jit(solution)/shard_map/ppermute | solution.py:274
  24.2 0.6 copy-start.4
  24.2 0.7 copy-start.5
  41.4 5.2 %collective-permute-start.4 = (bf16[16,80,256]{2,1,0:T(8,128)(2,1)}, bf16[16,80,256]{2,1,0:T(8,128)(2,1)S(1)}, u32[]{:S(2)}, u32[]{:S(2)}) collective-permute-start(bf16[16,80,256]{2,1,0:T(8,128)(2,1)} %get-tuple-element.11), channel_id=1, source_target_pairs={{0,1},{1,0},{2,3},{3,2},{4,5},{5,4},{6,7},{7,6},{8,9},{9,8},{10,11... | collective-permute-start | bytes 1966088 | tf_op jit(solution)/shard_map/ppermute | solution.py:331
  67.0 2.9 %collective-permute-start.7 = (bf16[80,256]{1,0:T(8,128)(2,1)S(1)}, bf16[80,256]{1,0:T(8,128)(2,1)S(1)}, u32[]{:S(2)}, u32[]{:S(2)}) collective-permute-start(bf16[80,256]{1,0:T(8,128)(2,1)S(1)} %reduce_sum.12), channel_id=1, source_target_pairs={{0,66},{2,0},{64,2},{66,64},{1,67},{3,1},{65,3},{67,65},{4,70},{6,... | collective-permute-start | bytes 122888 | tf_op jit(solution)/shard_map/ppermute | solution.py:338
  67.2 4.4 %collective-permute-start.6 = (bf16[80,256]{1,0:T(8,128)(2,1)S(1)}, bf16[80,256]{1,0:T(8,128)(2,1)S(1)}, u32[]{:S(2)}, u32[]{:S(2)}) collective-permute-start(bf16[80,256]{1,0:T(8,128)(2,1)S(1)} %reduce_sum.12), channel_id=1, source_target_pairs={{0,64},{2,66},{64,0},{66,2},{1,65},{3,67},{65,1},{67,3},{4,68},{6,... | collective-permute-start | bytes 122888 | tf_op jit(solution)/shard_map/ppermute | solution.py:338
  69.4 4.1 %collective-permute-start.5 = (bf16[80,256]{1,0:T(8,128)(2,1)S(1)}, bf16[80,256]{1,0:T(8,128)(2,1)S(1)}, u32[]{:S(2)}, u32[]{:S(2)}) collective-permute-start(bf16[80,256]{1,0:T(8,128)(2,1)S(1)} %reduce_sum.12), channel_id=1, source_target_pairs={{0,2},{2,64},{64,66},{66,0},{1,3},{3,65},{65,67},{67,1},{4,6},{6,6... | collective-permute-start | bytes 122888 | tf_op jit(solution)/shard_map/ppermute | solution.py:338
  73.4 13.7 %copy-start = (bf16[9,256,256]{2,1,0:T(8,128)(2,1)S(1)}, bf16[9,256,256]{2,1,0:T(8,128)(2,1)}, u32[]{:S(2)}) copy-start(bf16[9,256,256]{2,1,0:T(8,128)(2,1)} %param.5) | copy-start | bytes 3538948
  98.8 1.3 %slice-start = ((bf16[32,80,256]{2,1,0:T(8,128)(2,1)}), bf16[32,72,256]{2,1,0:T(8,128)(2,1)S(1)}, s32[]{:S(2)}) async-start(bf16[32,80,256]{2,1,0:T(8,128)(2,1)} %all-gather.2.cloned.1.call-done), calls=%async_computation.3 | async-start | bytes 2359296 | tf_op jit(solution)/shard_map/slice | solution.py:342
  100.1 1.7 %copy-start.1 = (bf16[32,80,256]{2,1,0:T(8,128)(2,1)S(1)}, bf16[32,80,256]{2,1,0:T(8,128)(2,1)}, u32[]{:S(2)}) copy-start(bf16[32,80,256]{2,1,0:T(8,128)(2,1)} %all-gather.2.cloned.1.call-done) | copy-start | bytes 3932164
Sparse Core Ops, SparseCore 0:
  87.2 11.5 all-gather.1

commit v2 on v1

--- a/solution.py
+++ b/solution.py
@@ -1,3 +1,4 @@
+import functools
 import math
 
 import jax
@@ -7,8 +8,10 @@
 from jax.experimental.pallas import tpu as pltpu
 from jax.sharding import Mesh, PartitionSpec as P
 
+
 F32 = jnp.float32
 BF16 = jnp.bfloat16
+HALVES = 2
 LAT = ("yh", "z")
 LON = ("x", "yl", "core")
 RING = ("yh", "yl")
@@ -74,7 +77,7 @@
         return acc + bias[...]
 
     def slope(pre):
-        sigma = 1.0 / (1.0 + jnp.exp(-pre))
+        sigma = 0.5 + 0.5 * jnp.tanh(0.5 * pre)
         return sigma, sigma * (1.0 + pre * (1.0 - sigma))
 
     def join(ref, slot, at):
@@ -116,7 +119,7 @@
         ]
         pre = conv(parts)
         sigma, rate = slope(pre)
-        active = (pre * sigma).astype(BF16).astype(F32).reshape(step, width, chans)
+        active = (pre * sigma).reshape(step, width, chans)
         rate = rate.reshape(step, width, chans)
         lines = []
         for m in range(step // 2):
@@ -138,7 +141,7 @@
         flipped[:, pl.ds(at, step * cols)] = own.T
         return carry
 
-    lax.fori_loop(0, batches * blocks, block, 0)
+    lax.fori_loop(0, batches * blocks, block, 0, unroll=True)
 
     size = rows * cols
     for r in range(3):
@@ -162,9 +165,13 @@
             ref[j, deep:, :] = tail.astype(ref.dtype)
 
 
-def back_kernel(flags, grad, weights, out, wide, ends, acc):
-    batches, slots, width, chans = grad.shape
+def back_kernel(part, halves, flags, grad, weights, *refs):
+    out, wide, end, lines_out, sem = refs[-5:]
+    slots, width, chans = grad.shape[1:]
     rows, cols = slots - 2, width - 8
+    deep = rows // halves
+    b, half = part // halves, part % halves
+    start = half * deep
     step = 8
     is_north, is_south = flags[0], flags[1]
 
@@ -174,38 +181,47 @@
         ref[(*index, slice(None), slice(chans, 2 * chans))] = line[:cols].astype(BF16)
         ref[(*index, slice(None), slice(2 * chans, 3 * chans))] = pltpu.roll(line, width - 1, 0)[:cols].astype(BF16)
 
-    for b in range(batches):
-        put(grad[b, 0], ends, (0, b))
-        put(grad[b, slots - 1], ends, (1, b))
-        wide[b, 0] = jnp.zeros_like(wide[b, 0])
-        wide[b, slots - 1] = jnp.zeros_like(wide[b, slots - 1])
-
-        def fill(i, carry):
-            put(grad[b, i + 1], wide, (b, i + 1))
-            return carry
-
-        lax.fori_loop(0, rows, fill, 0, unroll=4)
-
-    for t in range(2):
-        tap = jnp.where(is_north == 1, 0, 2) if t == 0 else jnp.where(is_south == 1, 2, 0)
-        lines = ends[t].reshape(batches * cols, 3 * chans)
-        acc[t] = jnp.dot(lines, weights[tap], preferred_element_type=F32).reshape(batches, cols, chans)
-
-    for b in range(batches):
-        for first in range(0, rows, step):
-            total = None
-            for r in range(3):
-                lines = wide[b, first + 2 - r : first + 2 - r + step, :, :].reshape(step * cols, 3 * chans)
-                term = jnp.dot(lines, weights[r], preferred_element_type=F32)
-                total = term if total is None else total + term
-            total = total.reshape(step, cols, chans)
-            for k in range(step):
-                line = total[k]
-                if first + k == 0:
-                    line = line + acc[0, b]
-                if first + k == rows - 1:
-                    line = line + acc[1, b]
-                out[b, first + k] = line.astype(BF16)
+    edges = []
+    for t, (own, slot, local_slot) in enumerate(((half == 0, 0, 0), (half == halves - 1, slots - 1, deep + 1))):
+        if own:
+            put(grad[b, slot], end, (t,))
+            wide[local_slot] = jnp.zeros_like(wide[local_slot])
+            tap = jnp.where(is_north == 1, 0, 2) if t == 0 else jnp.where(is_south == 1, 2, 0)
+            edges.append(jnp.dot(end[t], weights[tap], preferred_element_type=F32))
+        else:
+            edges.append(None)
+            put(grad[b, start + local_slot], wide, (local_slot,))
+    for k in range(1, deep + 1):
+        put(grad[b, start + k], wide, (k,))
+
+    for first in range(0, deep, step):
+        total = None
+        for r in range(3):
+            lines = wide[first + 2 - r : first + 2 - r + step, :, :].reshape(step * cols, 3 * chans)
+            term = jnp.dot(lines, weights[r], preferred_element_type=F32)
+            total = term if total is None else total + term
+        total = total.reshape(step, cols, chans)
+        for k in range(step):
+            line = total[k]
+            if first + k == 0 and edges[0] is not None:
+                line = line + edges[0]
+            if first + k == deep - 1 and edges[1] is not None:
+                line = line + edges[1]
+            lines_out[first + k] = line.astype(BF16)
+    copy = pltpu.make_async_copy(lines_out, out.at[b, start : start + deep], sem)
+    copy.start()
+    copy.wait()
+
+
+def finish_kernel(flags, mine, other, grad_kernel, grad_bias):
+    parts, deep = mine.shape[0], mine.shape[1] - 8
+    core = flags[3]
+    for ref, side in ((mine, core), (other, 1 - core)):
+        for j in range(parts):
+            at = pl.multiple_of((side * parts + j) * deep, 8)
+            grad_kernel[pl.ds(at, deep), :] = ref[j, :deep, :].astype(F32)
+    first = jnp.where(core == 0, mine[0, deep:, :].astype(F32), other[0, deep:, :].astype(F32))
+    grad_bias[...] = first[:1]
 
 
 def circle(lats, lons):
@@ -227,6 +243,10 @@
     )
 
 
+def near(x):
+    return pltpu.with_memory_space_constraint(x, pltpu.VMEM)
+
+
 def vmem():
     return pl.BlockSpec(memory_space=pltpu.VMEM)
 
@@ -287,16 +307,17 @@
 
     weights = kernel.reshape(3, 3 * chans, chans)
     back_weights = jnp.swapaxes(kernel.reshape(3, 3, chans, chans)[:, ::-1], 2, 3).reshape(3, 3 * chans, chans)
+    weights, back_weights, from_right = lax.optimization_barrier((weights, back_weights, from_right))
     plane = lax.axis_size(PLANE)
     deep = 9 * chans // (2 * plane)
     smem = pl.BlockSpec(memory_space=pltpu.SMEM)
-    message_type = jax.ShapeDtypeStruct((plane, deep + 8, chans), BF16)
+    message_type = pltpu.VMEM((plane, deep + 8, chans), BF16)
     count = from_right.shape[1]
     pooled, grad, keep, give = pl.pallas_call(
         forward_kernel,
         out_shape=(
             jax.ShapeDtypeStruct((batches, pairs, halves, chans), BF16),
-            jax.ShapeDtypeStruct((batches, rows + 2, cols + 8, chans), BF16),
+            pltpu.VMEM((batches, rows + 2, cols + 8, chans), BF16),
             message_type,
             message_type,
         ),
@@ -312,21 +333,39 @@
             pltpu.VMEM((9 * chans, chans), F32),
             pltpu.VMEM((8, chans), F32),
         ],
+        compiler_params=pltpu.CompilerParams(vmem_limit_bytes=56 << 20),
         name="forward",
-    )(flags, share, fields, from_fore, from_aft, from_right, from_left, cotangent, weights, conv_bias[None])
-
-    back = pl.pallas_call(
-        back_kernel,
-        out_shape=jax.ShapeDtypeStruct((batches, rows, cols, chans), BF16),
-        in_specs=[smem, vmem(), vmem()],
-        out_specs=vmem(),
-        scratch_shapes=[
-            pltpu.VMEM((batches, rows + 2, cols, 3 * chans), BF16),
-            pltpu.VMEM((2, batches, cols, 3 * chans), BF16),
-            pltpu.VMEM((2, batches, cols, chans), F32),
-        ],
-        name="back",
-    )(flags, grad, back_weights)
+    )(
+        flags, share, fields, near(from_fore), near(from_aft), near(from_right), near(from_left),
+        cotangent, weights, conv_bias[None],
+    )
+
+    parts_rows = rows // HALVES
+
+    def back_part(part, back):
+        held = () if back is None else (back,)
+        return pl.pallas_call(
+            functools.partial(back_kernel, part, HALVES),
+            out_shape=jax.ShapeDtypeStruct((batches, rows, cols, chans), BF16),
+            in_specs=[smem, vmem(), vmem()] + [pl.BlockSpec(memory_space=pl.ANY)] * len(held),
+            out_specs=pl.BlockSpec(memory_space=pl.ANY),
+            scratch_shapes=[
+                pltpu.VMEM((parts_rows + 2, cols, 3 * chans), BF16),
+                pltpu.VMEM((2, cols, 3 * chans), BF16),
+                pltpu.VMEM((parts_rows, cols, chans), BF16),
+                pltpu.SemaphoreType.DMA,
+            ],
+            input_output_aliases={3: 0} if held else {},
+            cost_estimate=pl.CostEstimate(
+                flops=2 * 9 * parts_rows * cols * chans * chans, transcendentals=0, bytes_accessed=parts_rows * cols * chans * 4
+            ),
+            compiler_params=pltpu.CompilerParams(vmem_limit_bytes=10 << 20),
+            name="back",
+        )(flags, near(grad), near(back_weights), *held)
+
+    back = None
+    for part in range(batches * HALVES):
+        back = back_part(part, back)
 
     take = lax.ppermute(give, "core", [(0, 1), (1, 0)])
     part = (keep.astype(F32) + take.astype(F32)).astype(BF16)
@@ -335,12 +374,21 @@
     size = lax.axis_size(RING)
     total = part.astype(F32)
     for k in range(1, size):
-        total = total + lax.ppermute(part, RING, [(i, (i + k) % size) for i in range(size)]).astype(F32)
+        away = lax.ppermute(part, RING, [(i, (i + k) % size) for i in range(size)])
+        total = total + away.astype(F32)
     total = jnp.broadcast_to(total.astype(BF16)[None], (plane, deep + 8, chans))
     total = lax.all_to_all(total, PLANE, 0, 0, tiled=True)
-    total = lax.all_gather(total, "core", axis=0, tiled=True)
-    grad_kernel = total[:, :deep].astype(F32).reshape(9, chans, chans)
-    grad_bias = total[0, deep].astype(F32)
+    other = lax.ppermute(total, "core", [(0, 1), (1, 0)])
+    grad_kernel, grad_bias = pl.pallas_call(
+        finish_kernel,
+        out_shape=(jax.ShapeDtypeStruct((9 * chans, chans), F32), jax.ShapeDtypeStruct((1, chans), F32)),
+        in_specs=[smem, vmem(), vmem()],
+        out_specs=[vmem()] * 2,
+        compiler_params=pltpu.CompilerParams(vmem_limit_bytes=10 << 20),
+        name="finish",
+    )(flags, near(total), near(other))
+    grad_kernel = grad_kernel.reshape(9, chans, chans)
+    grad_bias = grad_bias.reshape(chans)
     return pooled, back, grad_kernel, grad_bias
 
 

time: 110 us -> 95.2 us (0.87)
  between operations: 14.2 us -> 0.86 us
  starting transfers between devices: 13 us -> 19.8 us
  waiting for transfers between devices: 11 us -> 7.08 us
  local copies, waits for them, and re-layouts: 9.29 us -> 6.32 us
  other arithmetic: 4.84 us -> 2.58 us
    ppermute x3 -> x4, starting transfers between devices: 2.5 us -> 8.44 us  [the longest x3 4.64 us: local(): away = lax.ppermute(part, RING, [(i, (i + k) % size) for i in range(size)])]
    pallas_call x1 -> x5, Pallas kernels: 7.72 us -> 11.8 us  [the longest x4 9.71 us: back_part(): pl.pallas_call(functools.partial(back_kernel, part, HALVES), out_shape=ja...]
    pallas_call x1, Pallas kernels: 16.5 us -> 13.4 us  [local(): pl.pallas_call(forward_kernel, out_shape=(jax.ShapeDtypeStruct((batches,...]
    ppermute x1, starting transfers between devices: 0.07 us -> 2.52 us  [local(): from_fore = lax.ppermute(message(first_half), LAT + LON, fore)]
    ppermute x1, starting transfers between devices: 3.63 us -> 1.2 us  [local(): from_aft = lax.ppermute(message(~first_half), LAT + LON, aft)]
    all_gather x1 -> x0, waiting for transfers between devices: 2.15 us -> none  [local(): total = lax.all_gather(total, 'core', axis=0, tiled=True)]
    ppermute x1, waiting for transfers between devices: 1.94 us -> 0.01 us  [local(): from_fore = lax.ppermute(message(first_half), LAT + LON, fore)]
    reshape x1 -> x0, other arithmetic: 1.62 us -> none  [local(): grad_kernel = total[:, :deep].astype(F32).reshape(9, chans, chans)]
  transfers between devices with their start and end apart: 9 -> 9, of which waited for: 7 -> 5; matrix products, arithmetic and copies ran while one was open for 6% -> 5% of each run, Pallas kernels for 7% -> 10%
where the time goes in v2:
time: 95.2 us; the launch traced here: 94.9 us
  blocking collectives  32.9 us (35%)
  Pallas kernels  25.3 us (27%)
  starting transfers between devices  19.8 us (21%)
  waiting for transfers between devices  7.08 us (7%)
  local copies, waits for them, and re-layouts  6.32 us (7%)
  other arithmetic  2.58 us (3%)
    all_to_all x1, blocking collectives, local(): part = lax.all_to_all(part, PLANE, 0, 0, tiled=True)  19.8 us
    pallas_call x1, Pallas kernels, local(): pl.pallas_call(forward_kernel, out_shape=(jax.ShapeDtypeStruct((batches,...  13.4 us
    all_to_all x1, blocking collectives, local(): total = lax.all_to_all(total, PLANE, 0, 0, tiled=True)  13.1 us
    pallas_call x4, Pallas kernels, back_part(): pl.pallas_call(functools.partial(back_kernel, part, HALVES), out_shape=ja...  9.71 us
    ppermute x1, starting transfers between devices, local(): take = lax.ppermute(give, 'core', [(0, 1), (1, 0)])  4.74 us
    ppermute x3, starting transfers between devices, local(): away = lax.ppermute(part, RING, [(i, (i + k) % size) for i in range(size)])  4.64 us
    ppermute x1, starting transfers between devices, local(): other = lax.ppermute(total, 'core', [(0, 1), (1, 0)])  3.8 us
    ppermute x3, waiting for transfers between devices, local(): away = lax.ppermute(part, RING, [(i, (i + k) % size) for i in range(size)])  3.73 us
  transfers between devices with their start and end apart: 9, of which 5 were waited for; matrix products, arithmetic and copies ran while one was open for 5% of the time, Pallas kernels for 10%

profile of v2, /device:TPU:1, one launch (start us, length us, event | category | flops | bytes accessed | tf_op | source)
XLA Modules:
  0.0 94.9 jit_solution(3025275992288870303)
XLA Ops:
  0.7 0.9 dynamic-slice_bitcast_fusion
  1.5 0.9 constant_dynamic-slice_fusion.1
  2.5 2.5 %collective-permute-start = (bf16[2,120,256]{2,1,0:T(8,128)(2,1)S(1)}, bf16[2,120,256]{2,1,0:T(8,128)(2,1)S(1)}, u32[]{:S(2)}, u32[]{:S(2)}) collective-permute-start(bf16[2,120,256]{2,1,0:T(8,128)(2,1)S(1)} %pad_maximum_fusion), channel_id=1, source_target_pairs={{0,16},{1,17},{2,18},{3,19},{4,20},{5,21},{6,22},{7,23},{8,0},{9,1... | collective-permute-start | bytes 368648 | tf_op jit(solution)/shard_map/ppermute | solution.py:276
  5.0 1.2 %collective-permute-start.1 = (bf16[2,120,256]{2,1,0:T(8,128)(2,1)S(1)}, bf16[2,120,256]{2,1,0:T(8,128)(2,1)S(1)}, u32[]{:S(2)}, u32[]{:S(2)}) collective-permute-start(bf16[2,120,256]{2,1,0:T(8,128)(2,1)S(1)} %pad_maximum_fusion.1), channel_id=1, source_target_pairs={{16,0},{17,1},{18,2},{19,3},{20,4},{21,5},{22,6},{23,7},{0,8},{1,9... | collective-permute-start | bytes 368648 | tf_op jit(solution)/shard_map/ppermute | solution.py:277
  6.2 1.6 %fusion = (bf16[2,32,1,256]{3,2,1,0:T(2,128)(2,1)S(1)}, bf16[2,32,1,256]{3,2,1,0:T(2,128)(2,1)S(1)}, bf16[2,32,1,256]{3,2,1,0:T(2,128)(2,1)S(1)}, bf16[2,32,1,256]{3,2,1,0:T(2,128)(2,1)S(1)}) fusion(bf16[2,32,48,256]{3,2,1,0:T(8,128)(2,1)} %field.1), kind=kLoop, calls=%fused_computation.26 | loop fusion | bytes 262144 | tf_op jit(solution)/shard_map/slice | solution.py:283
  7.8 1.0 %fusion.1 = (bf16[2,16,1,256]{3,2,1,0:T(2,128)(2,1)S(1)}, bf16[2,16,1,256]{3,2,1,0:T(2,128)(2,1)S(1)}) fusion(bf16[2,16,24,256]{3,2,1,0:T(8,128)(2,1)} %cot.1), kind=kLoop, calls=%fused_computation.27 | loop fusion | bytes 65536 | tf_op jit(solution)/shard_map/slice | solution.py:289
  8.8 0.7 copy.11
  9.7 0.6 multiply_divide_fusion.share
  10.4 0.5 concatenate.22
  10.9 1.4 %collective-permute-start.2 = (bf16[2,90,256]{2,1,0:T(8,128)(2,1)S(1)}, bf16[2,90,256]{2,1,0:T(8,128)(2,1)S(1)}, u32[]{:S(2)}, u32[]{:S(2)}) collective-permute-start(bf16[2,90,256]{2,1,0:T(8,128)(2,1)S(1)} %concatenate.22), channel_id=1, source_target_pairs={{1,0},{2,1},{3,2},{4,3},{5,4},{6,5},{7,6},{8,7},{9,8},{10,9},{11,1... | collective-permute-start | bytes 276488 | tf_op jit(solution)/shard_map/ppermute | solution.py:295
  12.3 0.5 concatenate.23
  12.8 1.6 %collective-permute-start.3 = (bf16[2,90,256]{2,1,0:T(8,128)(2,1)S(1)}, bf16[2,90,256]{2,1,0:T(8,128)(2,1)S(1)}, u32[]{:S(2)}, u32[]{:S(2)}) collective-permute-start(bf16[2,90,256]{2,1,0:T(8,128)(2,1)S(1)} %concatenate.23), channel_id=1, source_target_pairs={{0,1},{1,2},{2,3},{3,4},{4,5},{5,6},{6,7},{7,8},{8,9},{9,10},{10,1... | collective-permute-start | bytes 276488 | tf_op jit(solution)/shard_map/ppermute | solution.py:294
  14.4 0.6 add_convert_fusion.2.flags
  15.0 0.9 collective-permute-done.2.from_right
  15.9 0.7 collective-permute-done.3.from_left
  16.6 13.4 %forward.1 = (bf16[2,16,24,256]{3,2,1,0:T(8,128)(2,1)}, bf16[2,34,56,256]{3,2,1,0:T(8,128)(2,1)S(1)}, bf16[16,80,256]{2,1,0:T(8,128)(2,1)S(1)}, bf16[16,80,256]{2,1,0:T(8,128)(2,1)S(1)}) custom-call(s32[4]{0:T(128)} %add_convert_fusion.2.flags, f32[34]{0:T(128)} %multiply_divide_fusion.share, bf16[2,32,48,256]{3,2,1,0:T(8,128)(2,1)} %field.1, ...), custom_call_target="tpu_custom_call" | custom-call | tf_op jit(solution)/shard_map/forward/pallas_call | solution.py:316
  30.0 4.7 %collective-permute-start.4 = (bf16[16,80,256]{2,1,0:T(8,128)(2,1)S(1)}, bf16[16,80,256]{2,1,0:T(8,128)(2,1)S(1)}, u32[]{:S(2)}, u32[]{:S(2)}) collective-permute-start(bf16[16,80,256]{2,1,0:T(8,128)(2,1)S(1)} %get-tuple-element.19), channel_id=1, source_target_pairs={{0,1},{1,0},{2,3},{3,2},{4,5},{5,4},{6,7},{7,6},{8,9},{9,8},{10,11... | collective-permute-start | bytes 1966088 | tf_op jit(solution)/shard_map/ppermute | solution.py:370
  34.7 1.7 %collective-permute-done.4 = bf16[16,80,256]{2,1,0:T(8,128)(2,1)S(1)} collective-permute-done((bf16[16,80,256]{2,1,0:T(8,128)(2,1)S(1)}, bf16[16,80,256]{2,1,0:T(8,128)(2,1)S(1)}, u32[]{:S(2)}, u32[]{:S(2)}) %collective-permute-start.4) | collective-permute-done | bytes 655392 | tf_op jit(solution)/shard_map/ppermute | solution.py:370
  36.6 19.8 %all_to_all.10 = bf16[16,80,256]{2,1,0:T(8,128)(2,1)} all-to-all(bf16[16,80,256]{2,1,0:T(8,128)(2,1)S(1)} %add_convert_fusion), channel_id=1, replica_groups=mesh['yh'=2,'z'=4,'x'=4,'yl'=2,'core'=2] {'x','z'}, dimensions={0} | all-to-all | bytes 1310720 | tf_op jit(solution)/shard_map/all_to_all | solution.py:372
  56.5 1.2 %reduce_sum.12 = bf16[80,256]{1,0:T(8,128)(2,1)S(1)} reduce(bf16[16,80,256]{2,1,0:T(8,128)(2,1)} %all_to_all.10, bf16[]{:T(256)} %constant.75.clone.1), dimensions={0}, to_apply=%region_0.1 | reduce | flops 307200 | bytes 696322 | tf_op jit(solution)/shard_map/reduce_sum | solution.py:373
  57.6 1.2 %collective-permute-start.7 = (bf16[80,256]{1,0:T(8,128)(2,1)S(1)}, bf16[80,256]{1,0:T(8,128)(2,1)S(1)}, u32[]{:S(2)}, u32[]{:S(2)}) collective-permute-start(bf16[80,256]{1,0:T(8,128)(2,1)S(1)} %reduce_sum.12), channel_id=1, source_target_pairs={{0,66},{2,0},{64,2},{66,64},{1,67},{3,1},{65,3},{67,65},{4,70},{6,... | collective-permute-start | bytes 122888 | tf_op jit(solution)/shard_map/ppermute | solution.py:377
  58.9 2.7 %collective-permute-start.6 = (bf16[80,256]{1,0:T(8,128)(2,1)S(1)}, bf16[80,256]{1,0:T(8,128)(2,1)S(1)}, u32[]{:S(2)}, u32[]{:S(2)}) collective-permute-start(bf16[80,256]{1,0:T(8,128)(2,1)S(1)} %reduce_sum.12), channel_id=1, source_target_pairs={{0,64},{2,66},{64,0},{66,2},{1,65},{3,67},{65,1},{67,3},{4,68},{6,... | collective-permute-start | bytes 122888 | tf_op jit(solution)/shard_map/ppermute | solution.py:377
  61.5 0.8 collective-permute-start.5
  62.3 0.9 collective-permute-done.6
  63.2 2.8 %collective-permute-done.5 = bf16[80,256]{1,0:T(8,128)(2,1)S(1)} collective-permute-done((bf16[80,256]{1,0:T(8,128)(2,1)S(1)}, bf16[80,256]{1,0:T(8,128)(2,1)S(1)}, u32[]{:S(2)}, u32[]{:S(2)}) %collective-permute-start.5) | collective-permute-done | bytes 40992 | tf_op jit(solution)/shard_map/ppermute | solution.py:377
  66.1 13.1 %all_to_all.11.mine = bf16[16,80,256]{2,1,0:T(8,128)(2,1)S(1)} all-to-all(bf16[16,80,256]{2,1,0:T(8,128)(2,1)S(1)} %broadcast_in_dim.10), channel_id=1, replica_groups=mesh['yh'=2,'z'=4,'x'=4,'yl'=2,'core'=2] {'x','z'}, dimensions={0} | all-to-all | bytes 1310720 | tf_op jit(solution)/shard_map/all_to_all | solution.py:380
  79.2 3.8 %collective-permute-start.8 = (bf16[16,80,256]{2,1,0:T(8,128)(2,1)S(1)}, bf16[16,80,256]{2,1,0:T(8,128)(2,1)S(1)}, u32[]{:S(2)}, u32[]{:S(2)}) collective-permute-start(bf16[16,80,256]{2,1,0:T(8,128)(2,1)S(1)} %all_to_all.11.mine), channel_id=1, source_target_pairs={{0,1},{1,0},{2,3},{3,2},{4,5},{5,4},{6,7},{7,6},{8,9},{9,8},{10,11... | collective-permute-start | bytes 1966088 | tf_op jit(solution)/shard_map/ppermute | solution.py:381
  83.0 2.4 %back.4.refs_0_ = bf16[2,32,48,256]{3,2,1,0:T(8,128)(2,1)} custom-call(s32[4]{0:T(128)S(1)} %copy-done, bf16[2,34,56,256]{3,2,1,0:T(8,128)(2,1)S(1)} %get-tuple-element.16.grad, bf16[3,768,256]{2,1,0:T(8,128)(2,1)S(1)} %bitcast.32), custom_call_target="tpu_custom_call" | custom-call | flops 905969664 | bytes 786432 | tf_op jit(solution)/shard_map/back/pallas_call | solution.py:347
  85.4 2.4 %back.5.refs_0_ = bf16[2,32,48,256]{3,2,1,0:T(8,128)(2,1)} custom-call(s32[4]{0:T(128)S(1)} %copy-done, bf16[2,34,56,256]{3,2,1,0:T(8,128)(2,1)S(1)} %get-tuple-element.16.grad, bf16[3,768,256]{2,1,0:T(8,128)(2,1)S(1)} %bitcast.33, bf16[2,32,48,256]{3,2,1,0:T(8,128)(2,1)} %back.4.refs_0_), custom_call_target="tpu_custom_call", output_to_operand_aliasing={{}: (3, {})} | custom-call | flops 905969664 | bytes 786432 | tf_op jit(solution)/shard_map/back/pallas_call | solution.py:347
  87.9 2.4 %back.6.refs_0_ = bf16[2,32,48,256]{3,2,1,0:T(8,128)(2,1)} custom-call(s32[4]{0:T(128)S(1)} %copy-done, bf16[2,34,56,256]{3,2,1,0:T(8,128)(2,1)S(1)} %get-tuple-element.16.grad, bf16[3,768,256]{2,1,0:T(8,128)(2,1)S(1)} %bitcast.34, bf16[2,32,48,256]{3,2,1,0:T(8,128)(2,1)} %back.5.refs_0_), custom_call_target="tpu_custom_call", output_to_operand_aliasing={{}: (3, {})} | custom-call | flops 905969664 | bytes 786432 | tf_op jit(solution)/shard_map/back/pallas_call | solution.py:347
  90.3 2.4 %back.7 = bf16[2,32,48,256]{3,2,1,0:T(8,128)(2,1)} custom-call(s32[4]{0:T(128)S(1)} %copy-done, bf16[2,34,56,256]{3,2,1,0:T(8,128)(2,1)S(1)} %get-tuple-element.16.grad, bf16[3,768,256]{2,1,0:T(8,128)(2,1)S(1)} %bitcast.35, bf16[2,32,48,256]{3,2,1,0:T(8,128)(2,1)} %back.6.refs_0_), custom_call_target="tpu_custom_call", output_to_operand_aliasing={{}: (3, {})} | custom-call | flops 905969664 | bytes 786432 | tf_op jit(solution)/shard_map/back/pallas_call | solution.py:347
  92.8 2.1 %finish.1 = (f32[2304,256]{1,0:T(8,128)}, f32[1,256]{1,0:T(1,128)}) custom-call(s32[4]{0:T(128)S(1)} %copy-done, bf16[16,80,256]{2,1,0:T(8,128)(2,1)S(1)} %all_to_all.11.mine, bf16[16,80,256]{2,1,0:T(8,128)(2,1)S(1)} %collective-permute-done.8.other), custom_call_target="tpu_custom_call" | custom-call | tf_op jit(solution)/shard_map/finish/pallas_call | solution.py:382
  (22 shorter events, 0.5 us)
Async XLA Ops:
  0.6 8.2 %copy-start.1 = (bf16[9,256,256]{2,1,0:T(8,128)(2,1)S(1)}, bf16[9,256,256]{2,1,0:T(8,128)(2,1)}, u32[]{:S(2)}) copy-start(bf16[9,256,256]{2,1,0:T(8,128)(2,1)} %param.5) | copy-start | bytes 3538948
  2.5 7.8 %collective-permute-start = (bf16[2,120,256]{2,1,0:T(8,128)(2,1)S(1)}, bf16[2,120,256]{2,1,0:T(8,128)(2,1)S(1)}, u32[]{:S(2)}, u32[]{:S(2)}) collective-permute-start(bf16[2,120,256]{2,1,0:T(8,128)(2,1)S(1)} %pad_maximum_fusion), channel_id=1, source_target_pairs={{0,16},{1,17},{2,18},{3,19},{4,20},{5,21},{6,22},{7,23},{8,0},{9,1... | collective-permute-start | bytes 368648 | tf_op jit(solution)/shard_map/ppermute | solution.py:276
  5.0 5.3 %collective-permute-start.1 = (bf16[2,120,256]{2,1,0:T(8,128)(2,1)S(1)}, bf16[2,120,256]{2,1,0:T(8,128)(2,1)S(1)}, u32[]{:S(2)}, u32[]{:S(2)}) collective-permute-start(bf16[2,120,256]{2,1,0:T(8,128)(2,1)S(1)} %pad_maximum_fusion.1), channel_id=1, source_target_pairs={{16,0},{17,1},{18,2},{19,3},{20,4},{21,5},{22,6},{23,7},{0,8},{1,9... | collective-permute-start | bytes 368648 | tf_op jit(solution)/shard_map/ppermute | solution.py:277
  10.9 5.0 %collective-permute-start.2 = (bf16[2,90,256]{2,1,0:T(8,128)(2,1)S(1)}, bf16[2,90,256]{2,1,0:T(8,128)(2,1)S(1)}, u32[]{:S(2)}, u32[]{:S(2)}) collective-permute-start(bf16[2,90,256]{2,1,0:T(8,128)(2,1)S(1)} %concatenate.22), channel_id=1, source_target_pairs={{1,0},{2,1},{3,2},{4,3},{5,4},{6,5},{7,6},{8,7},{9,8},{10,9},{11,1... | collective-permute-start | bytes 276488 | tf_op jit(solution)/shard_map/ppermute | solution.py:295
  12.8 3.7 %collective-permute-start.3 = (bf16[2,90,256]{2,1,0:T(8,128)(2,1)S(1)}, bf16[2,90,256]{2,1,0:T(8,128)(2,1)S(1)}, u32[]{:S(2)}, u32[]{:S(2)}) collective-permute-start(bf16[2,90,256]{2,1,0:T(8,128)(2,1)S(1)} %concatenate.23), channel_id=1, source_target_pairs={{0,1},{1,2},{2,3},{3,4},{4,5},{5,6},{6,7},{7,8},{8,9},{9,10},{10,1... | collective-permute-start | bytes 276488 | tf_op jit(solution)/shard_map/ppermute | solution.py:294
  30.0 6.5 %collective-permute-start.4 = (bf16[16,80,256]{2,1,0:T(8,128)(2,1)S(1)}, bf16[16,80,256]{2,1,0:T(8,128)(2,1)S(1)}, u32[]{:S(2)}, u32[]{:S(2)}) collective-permute-start(bf16[16,80,256]{2,1,0:T(8,128)(2,1)S(1)} %get-tuple-element.19), channel_id=1, source_target_pairs={{0,1},{1,0},{2,3},{3,2},{4,5},{5,4},{6,7},{7,6},{8,9},{9,8},{10,11... | collective-permute-start | bytes 1966088 | tf_op jit(solution)/shard_map/ppermute | solution.py:370
  56.5 26.6 %copy-start = (s32[4]{0:T(128)S(1)}, s32[4]{0:T(128)}, u32[]{:S(2)}) copy-start(s32[4]{0:T(128)} %add_convert_fusion.2.flags) | copy-start | bytes 52
  57.6 4.6 %collective-permute-start.7 = (bf16[80,256]{1,0:T(8,128)(2,1)S(1)}, bf16[80,256]{1,0:T(8,128)(2,1)S(1)}, u32[]{:S(2)}, u32[]{:S(2)}) collective-permute-start(bf16[80,256]{1,0:T(8,128)(2,1)S(1)} %reduce_sum.12), channel_id=1, source_target_pairs={{0,66},{2,0},{64,2},{66,64},{1,67},{3,1},{65,3},{67,65},{4,70},{6,... | collective-permute-start | bytes 122888 | tf_op jit(solution)/shard_map/ppermute | solution.py:377
  58.9 4.4 %collective-permute-start.6 = (bf16[80,256]{1,0:T(8,128)(2,1)S(1)}, bf16[80,256]{1,0:T(8,128)(2,1)S(1)}, u32[]{:S(2)}, u32[]{:S(2)}) collective-permute-start(bf16[80,256]{1,0:T(8,128)(2,1)S(1)} %reduce_sum.12), channel_id=1, source_target_pairs={{0,64},{2,66},{64,0},{66,2},{1,65},{3,67},{65,1},{67,3},{4,68},{6,... | collective-permute-start | bytes 122888 | tf_op jit(solution)/shard_map/ppermute | solution.py:377
  61.5 4.5 %collective-permute-start.5 = (bf16[80,256]{1,0:T(8,128)(2,1)S(1)}, bf16[80,256]{1,0:T(8,128)(2,1)S(1)}, u32[]{:S(2)}, u32[]{:S(2)}) collective-permute-start(bf16[80,256]{1,0:T(8,128)(2,1)S(1)} %reduce_sum.12), channel_id=1, source_target_pairs={{0,2},{2,64},{64,66},{66,0},{1,3},{3,65},{65,67},{67,1},{4,6},{6,6... | collective-permute-start | bytes 122888 | tf_op jit(solution)/shard_map/ppermute | solution.py:377
  79.2 13.5 %collective-permute-start.8 = (bf16[16,80,256]{2,1,0:T(8,128)(2,1)S(1)}, bf16[16,80,256]{2,1,0:T(8,128)(2,1)S(1)}, u32[]{:S(2)}, u32[]{:S(2)}) collective-permute-start(bf16[16,80,256]{2,1,0:T(8,128)(2,1)S(1)} %all_to_all.11.mine), channel_id=1, source_target_pairs={{0,1},{1,0},{2,3},{3,2},{4,5},{5,4},{6,7},{7,6},{8,9},{9,8},{10,11... | collective-permute-start | bytes 1966088 | tf_op jit(solution)/shard_map/ppermute | solution.py:381

commit v3 on v2

--- a/solution.py
+++ b/solution.py
@@ -166,7 +166,11 @@
 
 
 def back_kernel(part, halves, flags, grad, weights, *refs):
-    out, wide, end, lines_out, sem = refs[-5:]
+    last = part == grad.shape[0] * halves - 1
+    if last:
+        out, flushed, wide, end, sem = refs[-5:]
+    else:
+        out, wide, end = refs[-3:]
     slots, width, chans = grad.shape[1:]
     rows, cols = slots - 2, width - 8
     deep = rows // halves
@@ -174,6 +178,11 @@
     start = half * deep
     step = 8
     is_north, is_south = flags[0], flags[1]
+    copies = []
+    if last:
+        for n, at in enumerate(((slice(0, b),), (b, slice(0, start)))):
+            copies.append(pltpu.make_async_copy(out.at[at], flushed.at[at], sem.at[n]))
+            copies[-1].start()
 
     def put(line, ref, index):
         line = line.astype(F32)
@@ -207,21 +216,43 @@
                 line = line + edges[0]
             if first + k == deep - 1 and edges[1] is not None:
                 line = line + edges[1]
-            lines_out[first + k] = line.astype(BF16)
-    copy = pltpu.make_async_copy(lines_out, out.at[b, start : start + deep], sem)
-    copy.start()
-    copy.wait()
-
-
-def finish_kernel(flags, mine, other, grad_kernel, grad_bias):
+            out[b, start + first + k] = line.astype(BF16)
+    for copy in copies:
+        copy.wait()
+
+
+def sum_kernel(parts, out):
+    total = parts[0].astype(F32)
+    for k in range(1, parts.shape[0]):
+        total = total + parts[k].astype(F32)
+    out[...] = total.astype(out.dtype)
+
+
+def finish_kernel(flags, mine, other, back, flushed, grad_kernel, grad_bias, back_out, lines, sem):
     parts, deep = mine.shape[0], mine.shape[1] - 8
     core = flags[3]
-    for ref, side in ((mine, core), (other, 1 - core)):
-        for j in range(parts):
-            at = pl.multiple_of((side * parts + j) * deep, 8)
-            grad_kernel[pl.ds(at, deep), :] = ref[j, :deep, :].astype(F32)
+    at = (back.shape[0] - 1, slice(back.shape[1] // HALVES * (HALVES - 1), back.shape[1]))
+    copies = [pltpu.make_async_copy(back.at[at], back_out.at[at], sem.at[0])]
+    copies[0].start()
+    steps = 2
+    many = parts // steps
+    for n, (ref, side) in enumerate(((mine, core), (other, 1 - core))):
+        for k in range(steps):
+            first = n * parts + k * many
+            for j in range(many):
+                lines[(first + j) * deep : (first + j + 1) * deep, :] = ref[k * many + j, :deep, :].astype(F32)
+            at = pl.multiple_of((side * parts + k * many) * deep, 8)
+            copy = pltpu.make_async_copy(
+                lines.at[first * deep : (first + many) * deep],
+                grad_kernel.at[pl.ds(at, many * deep)],
+                sem.at[1 + n * steps + k],
+            )
+            copy.start()
+            copies.append(copy)
     first = jnp.where(core == 0, mine[0, deep:, :].astype(F32), other[0, deep:, :].astype(F32))
     grad_bias[...] = first[:1]
+    for copy in copies:
+        copy.wait()
 
 
 def circle(lats, lons):
@@ -342,35 +373,46 @@
 
     parts_rows = rows // HALVES
 
+    parts = batches * HALVES
+
     def back_part(part, back):
-        held = () if back is None else (back,)
+        held = () if back is None else (near(back),)
+        ends = part == parts - 1
+        result = pltpu.VMEM(fields.shape, BF16)
+        hbm = pl.BlockSpec(memory_space=pl.ANY)
         return pl.pallas_call(
             functools.partial(back_kernel, part, HALVES),
-            out_shape=jax.ShapeDtypeStruct((batches, rows, cols, chans), BF16),
-            in_specs=[smem, vmem(), vmem()] + [pl.BlockSpec(memory_space=pl.ANY)] * len(held),
-            out_specs=pl.BlockSpec(memory_space=pl.ANY),
+            out_shape=(result, jax.ShapeDtypeStruct(fields.shape, BF16)) if ends else result,
+            in_specs=[smem, vmem(), vmem()] + [vmem()] * len(held),
+            out_specs=(vmem(), hbm) if ends else vmem(),
             scratch_shapes=[
                 pltpu.VMEM((parts_rows + 2, cols, 3 * chans), BF16),
                 pltpu.VMEM((2, cols, 3 * chans), BF16),
-                pltpu.VMEM((parts_rows, cols, chans), BF16),
-                pltpu.SemaphoreType.DMA,
-            ],
+            ] + [pltpu.SemaphoreType.DMA((2,))] * ends,
             input_output_aliases={3: 0} if held else {},
+            compiler_params=pltpu.CompilerParams(vmem_limit_bytes=10 << 20),
             cost_estimate=pl.CostEstimate(
                 flops=2 * 9 * parts_rows * cols * chans * chans, transcendentals=0, bytes_accessed=parts_rows * cols * chans * 4
             ),
-            compiler_params=pltpu.CompilerParams(vmem_limit_bytes=10 << 20),
             name="back",
         )(flags, near(grad), near(back_weights), *held)
 
     back = None
-    for part in range(batches * HALVES):
+    for part in range(parts):
         back = back_part(part, back)
+    back, flushed = back
 
     take = lax.ppermute(give, "core", [(0, 1), (1, 0)])
     part = (keep.astype(F32) + take.astype(F32)).astype(BF16)
     part = lax.all_to_all(part, PLANE, 0, 0, tiled=True)
-    part = part.astype(F32).sum(axis=0).astype(BF16)
+    part = pl.pallas_call(
+        sum_kernel,
+        out_shape=jax.ShapeDtypeStruct(part.shape[1:], BF16),
+        in_specs=[vmem()],
+        out_specs=vmem(),
+        compiler_params=pltpu.CompilerParams(vmem_limit_bytes=10 << 20),
+        name="sum",
+    )(near(part))
     size = lax.axis_size(RING)
     total = part.astype(F32)
     for k in range(1, size):
@@ -379,14 +421,21 @@
     total = jnp.broadcast_to(total.astype(BF16)[None], (plane, deep + 8, chans))
     total = lax.all_to_all(total, PLANE, 0, 0, tiled=True)
     other = lax.ppermute(total, "core", [(0, 1), (1, 0)])
-    grad_kernel, grad_bias = pl.pallas_call(
+
+    grad_kernel, grad_bias, back = pl.pallas_call(
         finish_kernel,
-        out_shape=(jax.ShapeDtypeStruct((9 * chans, chans), F32), jax.ShapeDtypeStruct((1, chans), F32)),
-        in_specs=[smem, vmem(), vmem()],
-        out_specs=[vmem()] * 2,
+        out_shape=(
+            jax.ShapeDtypeStruct((9 * chans, chans), F32),
+            jax.ShapeDtypeStruct((1, chans), F32),
+            jax.ShapeDtypeStruct(fields.shape, BF16),
+        ),
+        in_specs=[smem] + [vmem()] * 3 + [pl.BlockSpec(memory_space=pl.ANY)],
+        out_specs=[pl.BlockSpec(memory_space=pl.ANY), vmem(), pl.BlockSpec(memory_space=pl.ANY)],
+        scratch_shapes=[pltpu.VMEM((9 * chans, chans), F32), pltpu.SemaphoreType.DMA((5,))],
+        input_output_aliases={4: 2},
         compiler_params=pltpu.CompilerParams(vmem_limit_bytes=10 << 20),
         name="finish",
-    )(flags, near(total), near(other))
+    )(flags, near(total), near(other), near(back), flushed)
     grad_kernel = grad_kernel.reshape(9, chans, chans)
     grad_bias = grad_bias.reshape(chans)
     return pooled, back, grad_kernel, grad_bias

time: 95.2 us -> 89.3 us (0.938)
  Pallas kernels: 25.3 us -> 22.9 us
  blocking collectives: 32.9 us -> 31.2 us
  starting transfers between devices: 19.8 us -> 18.5 us
  other arithmetic: 2.58 us -> 1.5 us
    pallas_call x4 -> x5, Pallas kernels: 9.71 us -> 6.79 us  [the longest x4 6.7 us: back_part(): pl.pallas_call(functools.partial(back_kernel, part, HALVES), out_shape=(r...]
    ppermute x1, starting transfers between devices: 2.52 us -> 0.07 us  [local(): from_fore = lax.ppermute(message(first_half), LAT + LON, fore)]
    ppermute x1, starting transfers between devices: 1.2 us -> 3.63 us  [local(): from_aft = lax.ppermute(message(~first_half), LAT + LON, aft)]
    ppermute x3, starting transfers between devices: 4.64 us -> 2.48 us  [local(): away = lax.ppermute(part, RING, [(i, (i + k) % size) for i in range(size)])]
    all_to_all x1, blocking collectives: 19.8 us -> 18.3 us  [local(): part = lax.all_to_all(part, PLANE, 0, 0, tiled=True)]
    reduce_sum x1 -> x0, other arithmetic: 1.18 us -> none  [local(): part = part.astype(F32).sum(axis=0).astype(BF16)]
    ppermute x1, waiting for transfers between devices: 0.01 us -> 1.16 us  [local(): from_fore = lax.ppermute(message(first_half), LAT + LON, fore)]
  transfers between devices with their start and end apart: 9 -> 9, of which waited for: 5 -> 7; matrix products, arithmetic and copies ran while one was open for 5% -> 6% of each run, Pallas kernels for 10% -> 8%
where the time goes in v3:
time: 89.3 us; the launch traced here: 89 us
  blocking collectives  31.2 us (35%)
  Pallas kernels  22.9 us (26%)
  starting transfers between devices  18.5 us (21%)
  waiting for transfers between devices  7.6 us (9%)
  local copies, waits for them, and re-layouts  6.29 us (7%)
  other arithmetic  1.5 us (2%)
  between operations  1.05 us (1%)
    all_to_all x1, blocking collectives, local(): part = lax.all_to_all(part, PLANE, 0, 0, tiled=True)  18.3 us
    pallas_call x1, Pallas kernels, local(): pl.pallas_call(forward_kernel, out_shape=(jax.ShapeDtypeStruct((batches,...  13.4 us
    all_to_all x1, blocking collectives, local(): total = lax.all_to_all(total, PLANE, 0, 0, tiled=True)  12.9 us
    pallas_call x4, Pallas kernels, back_part(): pl.pallas_call(functools.partial(back_kernel, part, HALVES), out_shape=(r...  6.7 us
    ppermute x1, starting transfers between devices, local(): other = lax.ppermute(total, 'core', [(0, 1), (1, 0)])  4.59 us
    ppermute x1, starting transfers between devices, local(): take = lax.ppermute(give, 'core', [(0, 1), (1, 0)])  4.15 us
    ppermute x3, waiting for transfers between devices, local(): away = lax.ppermute(part, RING, [(i, (i + k) % size) for i in range(size)])  3.72 us
    ppermute x1, starting transfers between devices, local(): from_aft = lax.ppermute(message(~first_half), LAT + LON, aft)  3.63 us
  transfers between devices with their start and end apart: 9, of which 7 were waited for; matrix products, arithmetic and copies ran while one was open for 6% of the time, Pallas kernels for 8%

profile of v3, /device:TPU:1, one launch (start us, length us, event | category | flops | bytes accessed | tf_op | source)
XLA Modules:
  0.0 89.0 jit_solution(17920431268850045497)
XLA Ops:
  0.7 0.9 dynamic-slice_bitcast_fusion
  1.5 0.9 constant_dynamic-slice_fusion.1
  2.5 3.6 %collective-permute-start.1 = (bf16[2,120,256]{2,1,0:T(8,128)(2,1)S(1)}, bf16[2,120,256]{2,1,0:T(8,128)(2,1)S(1)}, u32[]{:S(2)}, u32[]{:S(2)}) collective-permute-start(bf16[2,120,256]{2,1,0:T(8,128)(2,1)S(1)} %pad_maximum_fusion.1), channel_id=1, source_target_pairs={{16,0},{17,1},{18,2},{19,3},{20,4},{21,5},{22,6},{23,7},{0,8},{1,9... | collective-permute-start | bytes 368648 | tf_op jit(solution)/shard_map/ppermute | solution.py:308
  6.2 1.0 %fusion.1 = (bf16[2,16,1,256]{3,2,1,0:T(2,128)(2,1)S(1)}, bf16[2,16,1,256]{3,2,1,0:T(2,128)(2,1)S(1)}) fusion(bf16[2,16,24,256]{3,2,1,0:T(8,128)(2,1)} %cot.1), kind=kLoop, calls=%fused_computation.27 | loop fusion | bytes 65536 | tf_op jit(solution)/shard_map/slice | solution.py:320
  7.2 1.5 %fusion = (bf16[2,32,1,256]{3,2,1,0:T(2,128)(2,1)S(1)}, bf16[2,32,1,256]{3,2,1,0:T(2,128)(2,1)S(1)}, bf16[2,32,1,256]{3,2,1,0:T(2,128)(2,1)S(1)}, bf16[2,32,1,256]{3,2,1,0:T(2,128)(2,1)S(1)}) fusion(bf16[2,32,48,256]{3,2,1,0:T(8,128)(2,1)} %field.1), kind=kLoop, calls=%fused_computation.26 | loop fusion | bytes 262144 | tf_op jit(solution)/shard_map/slice | solution.py:314
  8.8 0.7 copy.12
  9.7 0.6 multiply_divide_fusion.share
  10.3 1.2 %collective-permute-done.from_fore = bf16[2,120,256]{2,1,0:T(8,128)(2,1)S(1)} collective-permute-done((bf16[2,120,256]{2,1,0:T(8,128)(2,1)S(1)}, bf16[2,120,256]{2,1,0:T(8,128)(2,1)S(1)}, u32[]{:S(2)}, u32[]{:S(2)}) %collective-permute-start) | collective-permute-done | bytes 122912 | tf_op jit(solution)/shard_map/ppermute | solution.py:307
  11.5 0.5 concatenate.22
  12.0 2.2 %collective-permute-start.2 = (bf16[2,90,256]{2,1,0:T(8,128)(2,1)S(1)}, bf16[2,90,256]{2,1,0:T(8,128)(2,1)S(1)}, u32[]{:S(2)}, u32[]{:S(2)}) collective-permute-start(bf16[2,90,256]{2,1,0:T(8,128)(2,1)S(1)} %concatenate.22), channel_id=1, source_target_pairs={{1,0},{2,1},{3,2},{4,3},{5,4},{6,5},{7,6},{8,7},{9,8},{10,9},{11,1... | collective-permute-start | bytes 276488 | tf_op jit(solution)/shard_map/ppermute | solution.py:326
  14.2 0.5 concatenate.23
  14.7 1.4 %collective-permute-start.3 = (bf16[2,90,256]{2,1,0:T(8,128)(2,1)S(1)}, bf16[2,90,256]{2,1,0:T(8,128)(2,1)S(1)}, u32[]{:S(2)}, u32[]{:S(2)}) collective-permute-start(bf16[2,90,256]{2,1,0:T(8,128)(2,1)S(1)} %concatenate.23), channel_id=1, source_target_pairs={{0,1},{1,2},{2,3},{3,4},{4,5},{5,6},{6,7},{7,8},{8,9},{9,10},{10,1... | collective-permute-start | bytes 276488 | tf_op jit(solution)/shard_map/ppermute | solution.py:325
  16.2 0.7 add_convert_fusion.2.flags
  16.8 0.9 collective-permute-done.2.from_right
  17.7 0.1 collective-permute-done.3.from_left
  17.8 13.4 %forward.1 = (bf16[2,16,24,256]{3,2,1,0:T(8,128)(2,1)}, bf16[2,34,56,256]{3,2,1,0:T(8,128)(2,1)S(1)}, bf16[16,80,256]{2,1,0:T(8,128)(2,1)S(1)}, bf16[16,80,256]{2,1,0:T(8,128)(2,1)S(1)}) custom-call(s32[4]{0:T(128)} %add_convert_fusion.2.flags, f32[34]{0:T(128)} %multiply_divide_fusion.share, bf16[2,32,48,256]{3,2,1,0:T(8,128)(2,1)} %field.1, ...), custom_call_target="tpu_custom_call" | custom-call | tf_op jit(solution)/shard_map/forward/pallas_call | solution.py:347
  31.2 4.2 %collective-permute-start.4 = (bf16[16,80,256]{2,1,0:T(8,128)(2,1)S(1)}, bf16[16,80,256]{2,1,0:T(8,128)(2,1)S(1)}, u32[]{:S(2)}, u32[]{:S(2)}) collective-permute-start(bf16[16,80,256]{2,1,0:T(8,128)(2,1)S(1)} %get-tuple-element.20), channel_id=1, source_target_pairs={{0,1},{1,0},{2,3},{3,2},{4,5},{5,4},{6,7},{7,6},{8,9},{9,8},{10,11... | collective-permute-start | bytes 1966088 | tf_op jit(solution)/shard_map/ppermute | solution.py:405
  35.4 1.7 %collective-permute-done.4 = bf16[16,80,256]{2,1,0:T(8,128)(2,1)S(1)} collective-permute-done((bf16[16,80,256]{2,1,0:T(8,128)(2,1)S(1)}, bf16[16,80,256]{2,1,0:T(8,128)(2,1)S(1)}, u32[]{:S(2)}, u32[]{:S(2)}) %collective-permute-start.4) | collective-permute-done | bytes 655392 | tf_op jit(solution)/shard_map/ppermute | solution.py:405
  37.1 0.2 add_convert_fusion
  37.3 18.3 %all_to_all.10.parts = bf16[16,80,256]{2,1,0:T(8,128)(2,1)S(1)} all-to-all(bf16[16,80,256]{2,1,0:T(8,128)(2,1)S(1)} %add_convert_fusion), channel_id=1, replica_groups=mesh['yh'=2,'z'=4,'x'=4,'yl'=2,'core'=2] {'x','z'}, dimensions={0} | all-to-all | bytes 1310720 | tf_op jit(solution)/shard_map/all_to_all | solution.py:407
  55.7 2.1 %collective-permute-start.6 = (bf16[80,256]{1,0:T(8,128)(2,1)S(1)}, bf16[80,256]{1,0:T(8,128)(2,1)S(1)}, u32[]{:S(2)}, u32[]{:S(2)}) collective-permute-start(bf16[80,256]{1,0:T(8,128)(2,1)S(1)} %sum.1), channel_id=1, source_target_pairs={{0,64},{2,66},{64,0},{66,2},{1,65},{3,67},{65,1},{67,3},{4,68},{6,... | collective-permute-start | bytes 122888 | tf_op jit(solution)/shard_map/ppermute | solution.py:419
  57.8 0.3 collective-permute-start.5
  58.1 0.4 collective-permute-done.7
  58.6 1.6 %collective-permute-done.6 = bf16[80,256]{1,0:T(8,128)(2,1)S(1)} collective-permute-done((bf16[80,256]{1,0:T(8,128)(2,1)S(1)}, bf16[80,256]{1,0:T(8,128)(2,1)S(1)}, u32[]{:S(2)}, u32[]{:S(2)}) %collective-permute-start.6) | collective-permute-done | bytes 40992 | tf_op jit(solution)/shard_map/ppermute | solution.py:419
  60.2 1.7 %collective-permute-done.5 = bf16[80,256]{1,0:T(8,128)(2,1)S(1)} collective-permute-done((bf16[80,256]{1,0:T(8,128)(2,1)S(1)}, bf16[80,256]{1,0:T(8,128)(2,1)S(1)}, u32[]{:S(2)}, u32[]{:S(2)}) %collective-permute-start.5) | collective-permute-done | bytes 40992 | tf_op jit(solution)/shard_map/ppermute | solution.py:419
  62.0 12.9 %all_to_all.11.mine = bf16[16,80,256]{2,1,0:T(8,128)(2,1)S(1)} all-to-all(bf16[16,80,256]{2,1,0:T(8,128)(2,1)S(1)} %broadcast_in_dim.10), channel_id=1, replica_groups=mesh['yh'=2,'z'=4,'x'=4,'yl'=2,'core'=2] {'x','z'}, dimensions={0} | all-to-all | bytes 1310720 | tf_op jit(solution)/shard_map/all_to_all | solution.py:422
  74.8 4.6 %collective-permute-start.8 = (bf16[16,80,256]{2,1,0:T(8,128)(2,1)S(1)}, bf16[16,80,256]{2,1,0:T(8,128)(2,1)S(1)}, u32[]{:S(2)}, u32[]{:S(2)}) collective-permute-start(bf16[16,80,256]{2,1,0:T(8,128)(2,1)S(1)} %all_to_all.11.mine), channel_id=1, source_target_pairs={{0,1},{1,0},{2,3},{3,2},{4,5},{5,4},{6,7},{7,6},{8,9},{9,8},{10,11... | collective-permute-start | bytes 1966088 | tf_op jit(solution)/shard_map/ppermute | solution.py:423
  79.4 1.7 %back.4.refs_0_ = bf16[2,32,48,256]{3,2,1,0:T(8,128)(2,1)S(1)} custom-call(s32[4]{0:T(128)S(1)} %copy-done, bf16[2,34,56,256]{3,2,1,0:T(8,128)(2,1)S(1)} %get-tuple-element.21.grad, bf16[3,768,256]{2,1,0:T(8,128)(2,1)S(1)} %bitcast.32), custom_call_target="tpu_custom_call" | custom-call | flops 905969664 | bytes 786432 | tf_op jit(solution)/shard_map/back/pallas_call | solution.py:383
  81.1 1.7 %back.5.refs_0_ = bf16[2,32,48,256]{3,2,1,0:T(8,128)(2,1)S(1)} custom-call(s32[4]{0:T(128)S(1)} %copy-done, bf16[2,34,56,256]{3,2,1,0:T(8,128)(2,1)S(1)} %get-tuple-element.21.grad, bf16[3,768,256]{2,1,0:T(8,128)(2,1)S(1)} %bitcast.33, bf16[2,32,48,256]{3,2,1,0:T(8,128)(2,1)S(1)} %back.4.refs_0_), custom_call_target="tpu_custom_call", output_to_operand_aliasing={{}: (3, {})} | custom-call | flops 905969664 | bytes 786432 | tf_op jit(solution)/shard_map/back/pallas_call | solution.py:383
  82.8 1.7 %back.6.refs_0_ = bf16[2,32,48,256]{3,2,1,0:T(8,128)(2,1)S(1)} custom-call(s32[4]{0:T(128)S(1)} %copy-done, bf16[2,34,56,256]{3,2,1,0:T(8,128)(2,1)S(1)} %get-tuple-element.21.grad, bf16[3,768,256]{2,1,0:T(8,128)(2,1)S(1)} %bitcast.34, bf16[2,32,48,256]{3,2,1,0:T(8,128)(2,1)S(1)} %back.5.refs_0_), custom_call_target="tpu_custom_call", output_to_operand_aliasing={{}: (3, {})} | custom-call | flops 905969664 | bytes 786432 | tf_op jit(solution)/shard_map/back/pallas_call | solution.py:383
  84.5 1.7 %back.7 = (bf16[2,32,48,256]{3,2,1,0:T(8,128)(2,1)S(1)}, bf16[2,32,48,256]{3,2,1,0:T(8,128)(2,1)}) custom-call(s32[4]{0:T(128)S(1)} %copy-done, bf16[2,34,56,256]{3,2,1,0:T(8,128)(2,1)S(1)} %get-tuple-element.21.grad, bf16[3,768,256]{2,1,0:T(8,128)(2,1)S(1)} %bitcast.35, bf16[2,32,48,256]{3,2,1,0:T(8,128)(2,1)S(1)} %back.6.refs_0_), custom_call_target="tpu_custom_call", output_to_operand_aliasing={{0}: (3, {})} | custom-call | flops 905969664 | bytes 786432 | tf_op jit(solution)/shard_map/back/pallas_call | solution.py:383
  86.2 2.7 %finish.1 = (f32[2304,256]{1,0:T(8,128)}, f32[1,256]{1,0:T(1,128)}, bf16[2,32,48,256]{3,2,1,0:T(8,128)(2,1)}) custom-call(s32[4]{0:T(128)S(1)} %copy-done, bf16[16,80,256]{2,1,0:T(8,128)(2,1)S(1)} %all_to_all.11.mine, bf16[16,80,256]{2,1,0:T(8,128)(2,1)S(1)} %collective-permute-done.8.other, ...), custom_call_target="tpu_custom_call", output_to_operand_aliasing={{2}: (4, {})} | custom-call | tf_op jit(solution)/shard_map/finish/pallas_call | solution.py:425
  (22 shorter events, 0.5 us)
Async XLA Ops:
  0.6 8.2 %copy-start.1 = (bf16[9,256,256]{2,1,0:T(8,128)(2,1)S(1)}, bf16[9,256,256]{2,1,0:T(8,128)(2,1)}, u32[]{:S(2)}) copy-start(bf16[9,256,256]{2,1,0:T(8,128)(2,1)} %param.5) | copy-start | bytes 3538948
  2.5 7.8 %collective-permute-start.1 = (bf16[2,120,256]{2,1,0:T(8,128)(2,1)S(1)}, bf16[2,120,256]{2,1,0:T(8,128)(2,1)S(1)}, u32[]{:S(2)}, u32[]{:S(2)}) collective-permute-start(bf16[2,120,256]{2,1,0:T(8,128)(2,1)S(1)} %pad_maximum_fusion.1), channel_id=1, source_target_pairs={{16,0},{17,1},{18,2},{19,3},{20,4},{21,5},{22,6},{23,7},{0,8},{1,9... | collective-permute-start | bytes 368648 | tf_op jit(solution)/shard_map/ppermute | solution.py:308
  6.1 5.3 %collective-permute-start = (bf16[2,120,256]{2,1,0:T(8,128)(2,1)S(1)}, bf16[2,120,256]{2,1,0:T(8,128)(2,1)S(1)}, u32[]{:S(2)}, u32[]{:S(2)}) collective-permute-start(bf16[2,120,256]{2,1,0:T(8,128)(2,1)S(1)} %pad_maximum_fusion), channel_id=1, source_target_pairs={{0,16},{1,17},{2,18},{3,19},{4,20},{5,21},{6,22},{7,23},{8,0},{9,1... | collective-permute-start | bytes 368648 | tf_op jit(solution)/shard_map/ppermute | solution.py:307
  12.0 5.7 %collective-permute-start.2 = (bf16[2,90,256]{2,1,0:T(8,128)(2,1)S(1)}, bf16[2,90,256]{2,1,0:T(8,128)(2,1)S(1)}, u32[]{:S(2)}, u32[]{:S(2)}) collective-permute-start(bf16[2,90,256]{2,1,0:T(8,128)(2,1)S(1)} %concatenate.22), channel_id=1, source_target_pairs={{1,0},{2,1},{3,2},{4,3},{5,4},{6,5},{7,6},{8,7},{9,8},{10,9},{11,1... | collective-permute-start | bytes 276488 | tf_op jit(solution)/shard_map/ppermute | solution.py:326
  14.7 3.1 %collective-permute-start.3 = (bf16[2,90,256]{2,1,0:T(8,128)(2,1)S(1)}, bf16[2,90,256]{2,1,0:T(8,128)(2,1)S(1)}, u32[]{:S(2)}, u32[]{:S(2)}) collective-permute-start(bf16[2,90,256]{2,1,0:T(8,128)(2,1)S(1)} %concatenate.23), channel_id=1, source_target_pairs={{0,1},{1,2},{2,3},{3,4},{4,5},{5,6},{6,7},{7,8},{8,9},{9,10},{10,1... | collective-permute-start | bytes 276488 | tf_op jit(solution)/shard_map/ppermute | solution.py:325
  31.2 5.9 %collective-permute-start.4 = (bf16[16,80,256]{2,1,0:T(8,128)(2,1)S(1)}, bf16[16,80,256]{2,1,0:T(8,128)(2,1)S(1)}, u32[]{:S(2)}, u32[]{:S(2)}) collective-permute-start(bf16[16,80,256]{2,1,0:T(8,128)(2,1)S(1)} %get-tuple-element.20), channel_id=1, source_target_pairs={{0,1},{1,0},{2,3},{3,2},{4,5},{5,4},{6,7},{7,6},{8,9},{9,8},{10,11... | collective-permute-start | bytes 1966088 | tf_op jit(solution)/shard_map/ppermute | solution.py:405
  55.6 23.9 %copy-start = (s32[4]{0:T(128)S(1)}, s32[4]{0:T(128)}, u32[]{:S(2)}) copy-start(s32[4]{0:T(128)} %add_convert_fusion.2.flags) | copy-start | bytes 52
  55.7 2.9 %collective-permute-start.7 = (bf16[80,256]{1,0:T(8,128)(2,1)S(1)}, bf16[80,256]{1,0:T(8,128)(2,1)S(1)}, u32[]{:S(2)}, u32[]{:S(2)}) collective-permute-start(bf16[80,256]{1,0:T(8,128)(2,1)S(1)} %sum.1), channel_id=1, source_target_pairs={{0,66},{2,0},{64,2},{66,64},{1,67},{3,1},{65,3},{67,65},{4,70},{6,... | collective-permute-start | bytes 122888 | tf_op jit(solution)/shard_map/ppermute | solution.py:419
  55.7 4.4 %collective-permute-start.6 = (bf16[80,256]{1,0:T(8,128)(2,1)S(1)}, bf16[80,256]{1,0:T(8,128)(2,1)S(1)}, u32[]{:S(2)}, u32[]{:S(2)}) collective-permute-start(bf16[80,256]{1,0:T(8,128)(2,1)S(1)} %sum.1), channel_id=1, source_target_pairs={{0,64},{2,66},{64,0},{66,2},{1,65},{3,67},{65,1},{67,3},{4,68},{6,... | collective-permute-start | bytes 122888 | tf_op jit(solution)/shard_map/ppermute | solution.py:419
  57.8 4.1 %collective-permute-start.5 = (bf16[80,256]{1,0:T(8,128)(2,1)S(1)}, bf16[80,256]{1,0:T(8,128)(2,1)S(1)}, u32[]{:S(2)}, u32[]{:S(2)}) collective-permute-start(bf16[80,256]{1,0:T(8,128)(2,1)S(1)} %sum.1), channel_id=1, source_target_pairs={{0,2},{2,64},{64,66},{66,0},{1,3},{3,65},{65,67},{67,1},{4,6},{6,6... | collective-permute-start | bytes 122888 | tf_op jit(solution)/shard_map/ppermute | solution.py:419
  74.8 11.3 %collective-permute-start.8 = (bf16[16,80,256]{2,1,0:T(8,128)(2,1)S(1)}, bf16[16,80,256]{2,1,0:T(8,128)(2,1)S(1)}, u32[]{:S(2)}, u32[]{:S(2)}) collective-permute-start(bf16[16,80,256]{2,1,0:T(8,128)(2,1)S(1)} %all_to_all.11.mine), channel_id=1, source_target_pairs={{0,1},{1,0},{2,3},{3,2},{4,5},{5,4},{6,7},{7,6},{8,9},{9,8},{10,11... | collective-permute-start | bytes 1966088 | tf_op jit(solution)/shard_map/ppermute | solution.py:423

commit v4 on v3

--- a/solution.py
+++ b/solution.py
@@ -27,12 +27,42 @@
     )
 
 
+def put_line(wide, b, e, line):
+    width, chans = line.shape
+    wide[b, e, :, :chans] = pltpu.roll(line, 1, 0).astype(BF16)
+    wide[b, e, :, chans : 2 * chans] = line.astype(BF16)
+    wide[b, e, :, 2 * chans :] = pltpu.roll(line, width - 1, 0).astype(BF16)
+
+
+def prepare_kernel(kernel, weights, back_weights):
+    chans = kernel.shape[-1]
+    for r in range(3):
+        for s in range(3):
+            tap = kernel[3 * r + s]
+            weights[r, s * chans : (s + 1) * chans, :] = tap
+            back_weights[r, (2 - s) * chans : (3 - s) * chans, :] = tap.T
+
+
+def fill_kernel(field, cot, wide, cot_out):
+    batches, rows, _, chans = field.shape
+    blank = jnp.zeros((8, chans), F32)
+    for b in range(batches):
+
+        def fill(i, carry):
+            put_line(wide, b, i + 2, jnp.concatenate([field[b, i].astype(F32), blank], axis=0))
+            return carry
+
+        lax.fori_loop(0, rows, fill, 0, unroll=4)
+    cot_out[...] = cot[...]
+
+
 def forward_kernel(
-    flags, share, field, from_fore, from_aft, from_right, from_left, cot, weights, bias,
+    flags, share, filled, from_fore, from_aft, from_right, from_left, cot, weights, bias,
     pooled, grad, keep, give, wide, right, left, spread, pool, flipped, total, bias_total,
 ):
-    batches, rows, cols, chans = field.shape
-    width = cols + 8
+    batches, slots, width, chans = wide.shape
+    chans //= 3
+    rows, cols = slots - 4, width - 8
     pairs = rows // 2
     step = 8
     is_north, is_south, first_half, core = flags[0], flags[1], flags[2], flags[3]
@@ -40,15 +70,29 @@
     left[...] = from_left[...].astype(F32)
     span = rows + 4
 
-    def put(b, e, own):
-        edge = edge_block(
+    place8 = lax.broadcasted_iota(jnp.int32, (8, chans), 0)
+
+    def edge_of(b, e):
+        return edge_block(
             right[b, pl.ds(e, 1), :], right[b, pl.ds(span + e, 1), :],
             left[b, pl.ds(e, 1), :], left[b, pl.ds(span + e, 1), :], chans,
         )
-        line = jnp.concatenate([own, edge], axis=0)
-        wide[b, e, :, :chans] = pltpu.roll(line, 1, 0).astype(BF16)
-        wide[b, e, :, chans : 2 * chans] = line.astype(BF16)
-        wide[b, e, :, 2 * chans :] = pltpu.roll(line, width - 1, 0).astype(BF16)
+
+    def put(b, e, own):
+        put_line(wide, b, e, jnp.concatenate([own, edge_of(b, e)], axis=0))
+
+    def patch(b, e):
+        edge = edge_of(b, e)
+        after, before = pltpu.roll(edge, 1, 0), pltpu.roll(edge, 7, 0)
+        low, high = wide[b, e, :16, chans : 2 * chans], wide[b, e, cols - 16 : cols, chans : 2 * chans]
+        up, down = wide[b, e, :16, :chans].astype(F32), wide[b, e, cols - 16 : cols, 2 * chans :].astype(F32)
+        wide[b, e, cols:, :chans] = jnp.where(place8 == 0, pltpu.roll(high.astype(F32)[8:], 1, 0), after).astype(BF16)
+        wide[b, e, cols:, chans : 2 * chans] = edge.astype(BF16)
+        wide[b, e, cols:, 2 * chans :] = jnp.where(place8 == 7, pltpu.roll(low.astype(F32)[:8], 7, 0), before).astype(BF16)
+        up = jnp.concatenate([jnp.where(place8 == 0, after, up[:8]), up[8:]], axis=0)
+        down = jnp.concatenate([down[:8], jnp.where(place8 == 7, before, down[8:])], axis=0)
+        wide[b, e, :16, :chans] = up.astype(BF16)
+        wide[b, e, cols - 16 : cols, 2 * chans :] = down.astype(BF16)
 
     def halo(b, lo, hi):
         fore = from_fore[b, lo:hi, :].astype(F32)
@@ -64,7 +108,7 @@
             put(b, rows + 2 + k, bottom)
 
         def fill(i, carry):
-            put(b, i + 2, field[b, i].astype(F32))
+            patch(b, i + 2)
             return carry
 
         lax.fori_loop(0, rows, fill, 0, unroll=4)
@@ -336,26 +380,42 @@
     core = lax.axis_index("core")
     flags = jnp.stack([is_north, is_south, first_half, core == 1]).astype(jnp.int32)
 
-    weights = kernel.reshape(3, 3 * chans, chans)
-    back_weights = jnp.swapaxes(kernel.reshape(3, 3, chans, chans)[:, ::-1], 2, 3).reshape(3, 3 * chans, chans)
-    weights, back_weights, from_right = lax.optimization_barrier((weights, back_weights, from_right))
+    weights_type = pltpu.VMEM((3, 3 * chans, chans), BF16)
+    weights, back_weights = pl.pallas_call(
+        prepare_kernel,
+        out_shape=(weights_type, weights_type),
+        in_specs=[vmem()],
+        out_specs=[vmem()] * 2,
+        compiler_params=pltpu.CompilerParams(vmem_limit_bytes=57 << 20),
+        name="prepare",
+    )(kernel)
     plane = lax.axis_size(PLANE)
     deep = 9 * chans // (2 * plane)
     smem = pl.BlockSpec(memory_space=pltpu.SMEM)
     message_type = pltpu.VMEM((plane, deep + 8, chans), BF16)
     count = from_right.shape[1]
-    pooled, grad, keep, give = pl.pallas_call(
+    wide_type = pltpu.VMEM((batches, rows + 4, cols + 8, 3 * chans), BF16)
+    wide, cot = pl.pallas_call(
+        fill_kernel,
+        out_shape=(wide_type, pltpu.VMEM(cotangent.shape, BF16)),
+        in_specs=[vmem()] * 2,
+        out_specs=[vmem()] * 2,
+        compiler_params=pltpu.CompilerParams(vmem_limit_bytes=52 << 20),
+        name="fill",
+    )(fields, cotangent)
+    pooled, grad, keep, give, _ = pl.pallas_call(
         forward_kernel,
         out_shape=(
             jax.ShapeDtypeStruct((batches, pairs, halves, chans), BF16),
             pltpu.VMEM((batches, rows + 2, cols + 8, chans), BF16),
             message_type,
             message_type,
+            wide_type,
         ),
         in_specs=[smem, smem] + [vmem()] * 8,
-        out_specs=[vmem()] * 4,
+        out_specs=[vmem()] * 5,
+        input_output_aliases={2: 4},
         scratch_shapes=[
-            pltpu.VMEM((batches, rows + 4, cols + 8, 3 * chans), BF16),
             pltpu.VMEM((batches, count, chans), F32),
             pltpu.VMEM((batches, count, chans), F32),
             pltpu.VMEM((4, chans // 128, cols, 128), F32),
@@ -364,11 +424,11 @@
             pltpu.VMEM((9 * chans, chans), F32),
             pltpu.VMEM((8, chans), F32),
         ],
-        compiler_params=pltpu.CompilerParams(vmem_limit_bytes=56 << 20),
+        compiler_params=pltpu.CompilerParams(vmem_limit_bytes=36 << 20),
         name="forward",
     )(
-        flags, share, fields, near(from_fore), near(from_aft), near(from_right), near(from_left),
-        cotangent, weights, conv_bias[None],
+        flags, share, near(wide), near(from_fore), near(from_aft), near(from_right), near(from_left),
+        near(cot), near(weights), conv_bias[None],
     )
 
     parts_rows = rows // HALVES

time: 89.3 us -> 94.2 us (1.055)
  local copies, waits for them, and re-layouts: 6.29 us -> 10.7 us
  Pallas kernels: 22.9 us -> 25 us
  other arithmetic: 1.5 us -> 0.43 us
    unnamed x6 -> x8, local copies, waits for them, and re-layouts: 0.02 us -> 5.4 us
    pallas_call x0 -> x2, Pallas kernels: none -> 3.83 us  [the longest x1 2.21 us: local(): pl.pallas_call(fill_kernel, out_shape=(wide_type, pltpu.VMEM(cotangent.sh...]
    pallas_call x1, Pallas kernels: 13.4 us -> 11.6 us  [local(): pl.pallas_call(forward_kernel, out_shape=(jax.ShapeDtypeStruct((batches,...]
    ppermute x1, starting transfers between devices: 4.15 us -> 5.36 us  [local(): take = lax.ppermute(give, 'core', [(0, 1), (1, 0)])]
    ppermute x1, waiting for transfers between devices: 1.16 us -> 0.01 us  [local(): from_fore = lax.ppermute(message(first_half), LAT + LON, fore)]
    ppermute x1, starting transfers between devices: 2.17 us -> 1.02 us  [local(): from_right = lax.ppermute(to_left, LON, [(j, i) for i, j in ring])]
  transfers between devices with their start and end apart: 9 -> 9, of which waited for: 7 -> 6; matrix products, arithmetic and copies ran while one was open for 6% -> 3% of each run, Pallas kernels for 8% -> 11%
where the time goes in v4:
time: 94.2 us; the launch traced here: 93.8 us
  blocking collectives  31.2 us (33%)
  Pallas kernels  25 us (27%)
  starting transfers between devices  17.8 us (19%)
  local copies, waits for them, and re-layouts  10.7 us (11%)
  waiting for transfers between devices  7.68 us (8%)
  between operations  1.04 us (1%)
    all_to_all x1, blocking collectives, local(): part = lax.all_to_all(part, PLANE, 0, 0, tiled=True)  18.1 us
    all_to_all x1, blocking collectives, local(): total = lax.all_to_all(total, PLANE, 0, 0, tiled=True)  13.1 us
    pallas_call x1, Pallas kernels, local(): pl.pallas_call(forward_kernel, out_shape=(jax.ShapeDtypeStruct((batches,...  11.6 us
    pallas_call x4, Pallas kernels, back_part(): pl.pallas_call(functools.partial(back_kernel, part, HALVES), out_shape=(r...  6.77 us
    unnamed x8, local copies, waits for them, and re-layouts  5.4 us
    ppermute x1, starting transfers between devices, local(): take = lax.ppermute(give, 'core', [(0, 1), (1, 0)])  5.36 us
    ppermute x1, starting transfers between devices, local(): other = lax.ppermute(total, 'core', [(0, 1), (1, 0)])  3.99 us
    ppermute x1, starting transfers between devices, local(): from_aft = lax.ppermute(message(~first_half), LAT + LON, aft)  3.63 us
  transfers between devices with their start and end apart: 9, of which 6 were waited for; matrix products, arithmetic and copies ran while one was open for 3% of the time, Pallas kernels for 11%

profile of v4, /device:TPU:1, one launch (start us, length us, event | category | flops | bytes accessed | tf_op | source)
XLA Modules:
  0.0 93.8 jit_solution(256276918320622993)
XLA Ops:
  0.7 0.8 dynamic-slice_bitcast_fusion
  1.4 0.9 constant_dynamic-slice_fusion.1
  2.4 3.6 %collective-permute-start.1 = (bf16[2,120,256]{2,1,0:T(8,128)(2,1)S(1)}, bf16[2,120,256]{2,1,0:T(8,128)(2,1)S(1)}, u32[]{:S(2)}, u32[]{:S(2)}) collective-permute-start(bf16[2,120,256]{2,1,0:T(8,128)(2,1)S(1)} %pad_maximum_fusion.1), channel_id=1, source_target_pairs={{16,0},{17,1},{18,2},{19,3},{20,4},{21,5},{22,6},{23,7},{0,8},{1,9... | collective-permute-start | bytes 368648 | tf_op jit(solution)/shard_map/ppermute | solution.py:352
  6.1 1.0 %fusion.1 = (bf16[2,16,1,256]{3,2,1,0:T(2,128)(2,1)S(1)}, bf16[2,16,1,256]{3,2,1,0:T(2,128)(2,1)S(1)}) fusion(bf16[2,16,24,256]{3,2,1,0:T(8,128)(2,1)} %cot.1), kind=kLoop, calls=%fused_computation.27 | loop fusion | bytes 65536 | tf_op jit(solution)/shard_map/slice | solution.py:364
  7.1 1.4 %fusion = (bf16[2,32,1,256]{3,2,1,0:T(2,128)(2,1)S(1)}, bf16[2,32,1,256]{3,2,1,0:T(2,128)(2,1)S(1)}, bf16[2,32,1,256]{3,2,1,0:T(2,128)(2,1)S(1)}, bf16[2,32,1,256]{3,2,1,0:T(2,128)(2,1)S(1)}) fusion(bf16[2,32,48,256]{3,2,1,0:T(8,128)(2,1)} %field.1), kind=kLoop, calls=%fused_computation.26 | loop fusion | bytes 262144 | tf_op jit(solution)/shard_map/slice | solution.py:358
  8.6 2.2 %fill.1 = (bf16[2,36,56,768]{3,2,1,0:T(8,128)(2,1)S(1)}, bf16[2,16,24,256]{3,2,1,0:T(8,128)(2,1)S(1)}) custom-call(bf16[2,32,48,256]{3,2,1,0:T(8,128)(2,1)} %field.1, bf16[2,16,24,256]{3,2,1,0:T(8,128)(2,1)} %cot.1), custom_call_target="tpu_custom_call" | custom-call | tf_op jit(solution)/shard_map/fill/pallas_call | solution.py:398
  10.9 2.6 %copy-done = bf16[2,36,56,768]{3,2,1,0:T(8,128)(2,1)} copy-done((bf16[2,36,56,768]{3,2,1,0:T(8,128)(2,1)}, bf16[2,36,56,768]{3,2,1,0:T(8,128)(2,1)S(1)}, u32[]{:S(2)}) %copy-start) | copy-done | bytes 6193176
  13.5 1.6 %prepare.1 = (bf16[3,768,256]{2,1,0:T(8,128)(2,1)S(1)}, bf16[3,768,256]{2,1,0:T(8,128)(2,1)S(1)}) custom-call(bf16[9,256,256]{2,1,0:T(8,128)(2,1)} %kernel.1), custom_call_target="tpu_custom_call" | custom-call | tf_op jit(solution)/shard_map/prepare/pallas_call | solution.py:384
  15.3 0.5 concatenate.22
  15.9 1.0 %collective-permute-start.2 = (bf16[2,90,256]{2,1,0:T(8,128)(2,1)S(1)}, bf16[2,90,256]{2,1,0:T(8,128)(2,1)S(1)}, u32[]{:S(2)}, u32[]{:S(2)}) collective-permute-start(bf16[2,90,256]{2,1,0:T(8,128)(2,1)S(1)} %concatenate.22), channel_id=1, source_target_pairs={{1,0},{2,1},{3,2},{4,3},{5,4},{6,5},{7,6},{8,7},{9,8},{10,9},{11,1... | collective-permute-start | bytes 276488 | tf_op jit(solution)/shard_map/ppermute | solution.py:370
  16.9 0.5 concatenate.23
  17.4 1.3 %collective-permute-start.3 = (bf16[2,90,256]{2,1,0:T(8,128)(2,1)S(1)}, bf16[2,90,256]{2,1,0:T(8,128)(2,1)S(1)}, u32[]{:S(2)}, u32[]{:S(2)}) collective-permute-start(bf16[2,90,256]{2,1,0:T(8,128)(2,1)S(1)} %concatenate.23), channel_id=1, source_target_pairs={{0,1},{1,2},{2,3},{3,4},{4,5},{5,6},{6,7},{7,8},{8,9},{9,10},{10,1... | collective-permute-start | bytes 276488 | tf_op jit(solution)/shard_map/ppermute | solution.py:369
  18.7 1.6 %collective-permute-done.2.from_right = bf16[2,90,256]{2,1,0:T(8,128)(2,1)S(1)} collective-permute-done((bf16[2,90,256]{2,1,0:T(8,128)(2,1)S(1)}, bf16[2,90,256]{2,1,0:T(8,128)(2,1)S(1)}, u32[]{:S(2)}, u32[]{:S(2)}) %collective-permute-start.2) | collective-permute-done | bytes 92192 | tf_op jit(solution)/shard_map/ppermute | solution.py:370
  20.4 1.0 %collective-permute-done.3.from_left = bf16[2,90,256]{2,1,0:T(8,128)(2,1)S(1)} collective-permute-done((bf16[2,90,256]{2,1,0:T(8,128)(2,1)S(1)}, bf16[2,90,256]{2,1,0:T(8,128)(2,1)S(1)}, u32[]{:S(2)}, u32[]{:S(2)}) %collective-permute-start.3) | collective-permute-done | bytes 92192 | tf_op jit(solution)/shard_map/ppermute | solution.py:369
  21.4 2.8 %copy-done.1 = bf16[2,36,56,768]{3,2,1,0:T(8,128)(2,1)S(1)} copy-done((bf16[2,36,56,768]{3,2,1,0:T(8,128)(2,1)S(1)}, bf16[2,36,56,768]{3,2,1,0:T(8,128)(2,1)}, u32[]{:S(2)}) %copy-start.1) | copy-done | bytes 6193176
  24.2 11.6 %forward.1 = (bf16[2,16,24,256]{3,2,1,0:T(8,128)(2,1)}, bf16[2,34,56,256]{3,2,1,0:T(8,128)(2,1)S(1)}, bf16[16,80,256]{2,1,0:T(8,128)(2,1)S(1)}, bf16[16,80,256]{...) custom-call(s32[4]{0:T(128)S(1)} %add_convert_fusion.2.flags, ...), custom_call_target="tpu_custom_call", output_to_operand_aliasing={{4}: (2, {})} | custom-call | tf_op jit(solution)/shard_map/forward/pallas_call | solution.py:406
  35.8 5.4 %collective-permute-start.4 = (bf16[16,80,256]{2,1,0:T(8,128)(2,1)S(1)}, bf16[16,80,256]{2,1,0:T(8,128)(2,1)S(1)}, u32[]{:S(2)}, u32[]{:S(2)}) collective-permute-start(bf16[16,80,256]{2,1,0:T(8,128)(2,1)S(1)} %get-tuple-element.22), channel_id=1, source_target_pairs={{0,1},{1,0},{2,3},{3,2},{4,5},{5,4},{6,7},{7,6},{8,9},{9,8},{10,11... | collective-permute-start | bytes 1966088 | tf_op jit(solution)/shard_map/ppermute | solution.py:465
  41.2 1.7 %collective-permute-done.4 = bf16[16,80,256]{2,1,0:T(8,128)(2,1)S(1)} collective-permute-done((bf16[16,80,256]{2,1,0:T(8,128)(2,1)S(1)}, bf16[16,80,256]{2,1,0:T(8,128)(2,1)S(1)}, u32[]{:S(2)}, u32[]{:S(2)}) %collective-permute-start.4) | collective-permute-done | bytes 655392 | tf_op jit(solution)/shard_map/ppermute | solution.py:465
  42.9 0.2 add_convert_fusion
  43.1 18.1 %all_to_all.10.parts = bf16[16,80,256]{2,1,0:T(8,128)(2,1)S(1)} all-to-all(bf16[16,80,256]{2,1,0:T(8,128)(2,1)S(1)} %add_convert_fusion), channel_id=1, replica_groups=mesh['yh'=2,'z'=4,'x'=4,'yl'=2,'core'=2] {'x','z'}, dimensions={0} | all-to-all | bytes 1310720 | tf_op jit(solution)/shard_map/all_to_all | solution.py:467
  61.3 1.6 %collective-permute-start.6 = (bf16[80,256]{1,0:T(8,128)(2,1)S(1)}, bf16[80,256]{1,0:T(8,128)(2,1)S(1)}, u32[]{:S(2)}, u32[]{:S(2)}) collective-permute-start(bf16[80,256]{1,0:T(8,128)(2,1)S(1)} %sum.1), channel_id=1, source_target_pairs={{0,64},{2,66},{64,0},{66,2},{1,65},{3,67},{65,1},{67,3},{4,68},{6,... | collective-permute-start | bytes 122888 | tf_op jit(solution)/shard_map/ppermute | solution.py:479
  62.9 0.8 collective-permute-start.5
  63.7 0.5 collective-permute-done.7
  64.2 1.6 %collective-permute-done.6 = bf16[80,256]{1,0:T(8,128)(2,1)S(1)} collective-permute-done((bf16[80,256]{1,0:T(8,128)(2,1)S(1)}, bf16[80,256]{1,0:T(8,128)(2,1)S(1)}, u32[]{:S(2)}, u32[]{:S(2)}) %collective-permute-start.6) | collective-permute-done | bytes 40992 | tf_op jit(solution)/shard_map/ppermute | solution.py:479
  65.8 1.2 %collective-permute-done.5 = bf16[80,256]{1,0:T(8,128)(2,1)S(1)} collective-permute-done((bf16[80,256]{1,0:T(8,128)(2,1)S(1)}, bf16[80,256]{1,0:T(8,128)(2,1)S(1)}, u32[]{:S(2)}, u32[]{:S(2)}) %collective-permute-start.5) | collective-permute-done | bytes 40992 | tf_op jit(solution)/shard_map/ppermute | solution.py:479
  67.1 13.1 %all_to_all.11.mine = bf16[16,80,256]{2,1,0:T(8,128)(2,1)S(1)} all-to-all(bf16[16,80,256]{2,1,0:T(8,128)(2,1)S(1)} %broadcast_in_dim.10), channel_id=1, replica_groups=mesh['yh'=2,'z'=4,'x'=4,'yl'=2,'core'=2] {'x','z'}, dimensions={0} | all-to-all | bytes 1310720 | tf_op jit(solution)/shard_map/all_to_all | solution.py:482
  80.2 4.0 %collective-permute-start.8 = (bf16[16,80,256]{2,1,0:T(8,128)(2,1)S(1)}, bf16[16,80,256]{2,1,0:T(8,128)(2,1)S(1)}, u32[]{:S(2)}, u32[]{:S(2)}) collective-permute-start(bf16[16,80,256]{2,1,0:T(8,128)(2,1)S(1)} %all_to_all.11.mine), channel_id=1, source_target_pairs={{0,1},{1,0},{2,3},{3,2},{4,5},{5,4},{6,7},{7,6},{8,9},{9,8},{10,11... | collective-permute-start | bytes 1966088 | tf_op jit(solution)/shard_map/ppermute | solution.py:483
  84.1 1.7 %back.4.refs_0_ = bf16[2,32,48,256]{3,2,1,0:T(8,128)(2,1)S(1)} custom-call(s32[4]{0:T(128)S(1)} %add_convert_fusion.2.flags, bf16[2,34,56,256]{3,2,1,0:T(8,128)(2,1)S(1)} %get-tuple-element.23.grad, bf16[3,768,256]{2,1,0:T(8,128)(2,1)S(1)} %get-tuple-element.24.weights), custom_call_target="tpu_custom_call" | custom-call | flops 905969664 | bytes 786432 | tf_op jit(solution)/shard_map/back/pallas_call | solution.py:443
  85.8 1.7 %back.5.refs_0_ = bf16[2,32,48,256]{3,2,1,0:T(8,128)(2,1)S(1)} custom-call(s32[4]{0:T(128)S(1)} %add_convert_fusion.2.flags, bf16[2,34,56,256]{3,2,1,0:T(8,128)(2,1)S(1)} %get-tuple-element.23.grad, bf16[3,768,256]{2,1,0:T(8,128)(2,1)S(1)} %get-tuple-element.24.weights, bf16[2,32,48,256]{3,2,1,0:T(8,128)(2,1)S(1)} %back.4.refs_0_), custom_call_target="tpu_custom_call", output_to_operand_aliasing={{}: (3, {})} | custom-call | flops 905969664 | bytes 786432 | tf_op jit(solution)/shard_map/back/pallas_call | solution.py:443
  87.5 1.7 %back.6.refs_0_ = bf16[2,32,48,256]{3,2,1,0:T(8,128)(2,1)S(1)} custom-call(s32[4]{0:T(128)S(1)} %add_convert_fusion.2.flags, bf16[2,34,56,256]{3,2,1,0:T(8,128)(2,1)S(1)} %get-tuple-element.23.grad, bf16[3,768,256]{2,1,0:T(8,128)(2,1)S(1)} %get-tuple-element.24.weights, bf16[2,32,48,256]{3,2,1,0:T(8,128)(2,1)S(1)} %back.5.refs_0_), custom_call_target="tpu_custom_call", output_to_operand_aliasing={{}: (3, {})} | custom-call | flops 905969664 | bytes 786432 | tf_op jit(solution)/shard_map/back/pallas_call | solution.py:443
  89.2 1.7 %back.7 = (bf16[2,32,48,256]{3,2,1,0:T(8,128)(2,1)S(1)}, bf16[2,32,48,256]{3,2,1,0:T(8,128)(2,1)}) custom-call(s32[4]{0:T(128)S(1)} %add_convert_fusion.2.flags, bf16[2,34,56,256]{3,2,1,0:T(8,128)(2,1)S(1)} %get-tuple-element.23.grad, bf16[3,768,256]{2,1,0:T(8,128)(2,1)S(1)} %get-tuple-element.24.weights, ...), custom_call_target="tpu_custom_call", output_to_operand_aliasing={{0}: (3, {})} | custom-call | flops 905969664 | bytes 786432 | tf_op jit(solution)/shard_map/back/pallas_call | solution.py:443
  91.0 2.7 %finish.1 = (f32[2304,256]{1,0:T(8,128)}, f32[1,256]{1,0:T(1,128)}, bf16[2,32,48,256]{3,2,1,0:T(8,128)(2,1)}) custom-call(s32[4]{0:T(128)S(1)} %add_convert_fusion.2.flags, bf16[16,80,256]{2,1,0:T(8,128)(2,1)S(1)} %all_to_all.11.mine, bf16[16,80,256]{2,1,0:T(8,128)(2,1)S(1)} %collective-permute-done.8.other, ...), custom_call_target="tpu_custom_call", output_to_operand_aliasing={{2}: (4, {})} | custom-call | tf_op jit(solution)/shard_map/finish/pallas_call | solution.py:485
  (24 shorter events, 0.6 us)
Async XLA Ops:
  2.4 12.8 %collective-permute-start.1 = (bf16[2,120,256]{2,1,0:T(8,128)(2,1)S(1)}, bf16[2,120,256]{2,1,0:T(8,128)(2,1)S(1)}, u32[]{:S(2)}, u32[]{:S(2)}) collective-permute-start(bf16[2,120,256]{2,1,0:T(8,128)(2,1)S(1)} %pad_maximum_fusion.1), channel_id=1, source_target_pairs={{16,0},{17,1},{18,2},{19,3},{20,4},{21,5},{22,6},{23,7},{0,8},{1,9... | collective-permute-start | bytes 368648 | tf_op jit(solution)/shard_map/ppermute | solution.py:352
  6.0 9.2 %collective-permute-start = (bf16[2,120,256]{2,1,0:T(8,128)(2,1)S(1)}, bf16[2,120,256]{2,1,0:T(8,128)(2,1)S(1)}, u32[]{:S(2)}, u32[]{:S(2)}) collective-permute-start(bf16[2,120,256]{2,1,0:T(8,128)(2,1)S(1)} %pad_maximum_fusion), channel_id=1, source_target_pairs={{0,16},{1,17},{2,18},{3,19},{4,20},{5,21},{6,22},{7,23},{8,0},{9,1... | collective-permute-start | bytes 368648 | tf_op jit(solution)/shard_map/ppermute | solution.py:351
  10.8 2.6 %copy-start = (bf16[2,36,56,768]{3,2,1,0:T(8,128)(2,1)}, bf16[2,36,56,768]{3,2,1,0:T(8,128)(2,1)S(1)}, u32[]{:S(2)}) copy-start(bf16[2,36,56,768]{3,2,1,0:T(8,128)(2,1)S(1)} %get-tuple-element.17.filled) | copy-start | bytes 18579460
  13.5 7.9 %copy-start.2 = (f32[256]{0:T(256)S(1)}, f32[256]{0:T(256)}, u32[]{:S(2)}) copy-start(f32[256]{0:T(256)} %param.6) | copy-start | bytes 3076
  15.9 4.5 %collective-permute-start.2 = (bf16[2,90,256]{2,1,0:T(8,128)(2,1)S(1)}, bf16[2,90,256]{2,1,0:T(8,128)(2,1)S(1)}, u32[]{:S(2)}, u32[]{:S(2)}) collective-permute-start(bf16[2,90,256]{2,1,0:T(8,128)(2,1)S(1)} %concatenate.22), channel_id=1, source_target_pairs={{1,0},{2,1},{3,2},{4,3},{5,4},{6,5},{7,6},{8,7},{9,8},{10,9},{11,1... | collective-permute-start | bytes 276488 | tf_op jit(solution)/shard_map/ppermute | solution.py:370
  17.4 4.0 %collective-permute-start.3 = (bf16[2,90,256]{2,1,0:T(8,128)(2,1)S(1)}, bf16[2,90,256]{2,1,0:T(8,128)(2,1)S(1)}, u32[]{:S(2)}, u32[]{:S(2)}) collective-permute-start(bf16[2,90,256]{2,1,0:T(8,128)(2,1)S(1)} %concatenate.23), channel_id=1, source_target_pairs={{0,1},{1,2},{2,3},{3,4},{4,5},{5,6},{6,7},{7,8},{8,9},{9,10},{10,1... | collective-permute-start | bytes 276488 | tf_op jit(solution)/shard_map/ppermute | solution.py:369
  21.4 2.8 %copy-start.1 = (bf16[2,36,56,768]{3,2,1,0:T(8,128)(2,1)S(1)}, bf16[2,36,56,768]{3,2,1,0:T(8,128)(2,1)}, u32[]{:S(2)}) copy-start(bf16[2,36,56,768]{3,2,1,0:T(8,128)(2,1)} %copy-done) | copy-start | bytes 18579460
  35.8 7.1 %collective-permute-start.4 = (bf16[16,80,256]{2,1,0:T(8,128)(2,1)S(1)}, bf16[16,80,256]{2,1,0:T(8,128)(2,1)S(1)}, u32[]{:S(2)}, u32[]{:S(2)}) collective-permute-start(bf16[16,80,256]{2,1,0:T(8,128)(2,1)S(1)} %get-tuple-element.22), channel_id=1, source_target_pairs={{0,1},{1,0},{2,3},{3,2},{4,5},{5,4},{6,7},{7,6},{8,9},{9,8},{10,11... | collective-permute-start | bytes 1966088 | tf_op jit(solution)/shard_map/ppermute | solution.py:465
  61.2 2.9 %collective-permute-start.7 = (bf16[80,256]{1,0:T(8,128)(2,1)S(1)}, bf16[80,256]{1,0:T(8,128)(2,1)S(1)}, u32[]{:S(2)}, u32[]{:S(2)}) collective-permute-start(bf16[80,256]{1,0:T(8,128)(2,1)S(1)} %sum.1), channel_id=1, source_target_pairs={{0,66},{2,0},{64,2},{66,64},{1,67},{3,1},{65,3},{67,65},{4,70},{6,... | collective-permute-start | bytes 122888 | tf_op jit(solution)/shard_map/ppermute | solution.py:479
  61.3 4.4 %collective-permute-start.6 = (bf16[80,256]{1,0:T(8,128)(2,1)S(1)}, bf16[80,256]{1,0:T(8,128)(2,1)S(1)}, u32[]{:S(2)}, u32[]{:S(2)}) collective-permute-start(bf16[80,256]{1,0:T(8,128)(2,1)S(1)} %sum.1), channel_id=1, source_target_pairs={{0,64},{2,66},{64,0},{66,2},{1,65},{3,67},{65,1},{67,3},{4,68},{6,... | collective-permute-start | bytes 122888 | tf_op jit(solution)/shard_map/ppermute | solution.py:479
  62.9 4.1 %collective-permute-start.5 = (bf16[80,256]{1,0:T(8,128)(2,1)S(1)}, bf16[80,256]{1,0:T(8,128)(2,1)S(1)}, u32[]{:S(2)}, u32[]{:S(2)}) collective-permute-start(bf16[80,256]{1,0:T(8,128)(2,1)S(1)} %sum.1), channel_id=1, source_target_pairs={{0,2},{2,64},{64,66},{66,0},{1,3},{3,65},{65,67},{67,1},{4,6},{6,6... | collective-permute-start | bytes 122888 | tf_op jit(solution)/shard_map/ppermute | solution.py:479
  80.2 10.8 %collective-permute-start.8 = (bf16[16,80,256]{2,1,0:T(8,128)(2,1)S(1)}, bf16[16,80,256]{2,1,0:T(8,128)(2,1)S(1)}, u32[]{:S(2)}, u32[]{:S(2)}) collective-permute-start(bf16[16,80,256]{2,1,0:T(8,128)(2,1)S(1)} %all_to_all.11.mine), channel_id=1, source_target_pairs={{0,1},{1,0},{2,3},{3,2},{4,5},{5,4},{6,7},{7,6},{8,9},{9,8},{10,11... | collective-permute-start | bytes 1966088 | tf_op jit(solution)/shard_map/ppermute | solution.py:483
